TPU v7x, 128 devices: a whole 4x4x4 slice. The times are simulated.
128 devices in a mesh: dp: 32 (over y, x, core), tensor: 4 (over z).
Axes of the slice: x: 4, y: 4, z: 4, core: 2. Of those that a mesh axis runs over, the one named last changes fastest.
Arguments:
- grad_query: bfloat16 [32, 8, 256, 2048], P('dp', None, None, 'tensor')
- grad_output: bfloat16 [32, 8, 256, 2048], P('dp', 'tensor')
- query_master: float32 [8, 256, 2048], P(None, 'dp', 'tensor'), may hold values from -4 to 4
- output_master: float32 [8, 256, 2048], P('tensor', 'dp'), may hold values from -4 to 4
- query_moment: float32 [8, 256, 2048], P(None, 'dp', 'tensor'), may hold values from 0.05 to 1
- output_moment: float32 [8, 256, 2048], P('tensor', 'dp'), may hold values from 0.05 to 1
- left_stat: float32 [4, 32, 3, 256, 256], P('tensor', 'dp')
- right_stat: float32 [4, 32, 3, 256, 256], P('tensor', 'dp')
- left_root: float32 [4, 32, 3, 256, 256], P('tensor', 'dp')
- right_root: float32 [4, 32, 3, 256, 256], P('tensor', 'dp')
- owner: int32 [4, 32], P('tensor'), may hold values from 0 to 31, as said below
Outputs:
- master_query: float32 [8, 256, 2048], P(None, 'dp', 'tensor')
- master_output: float32 [8, 256, 2048], P('tensor', 'dp')
- moment_query: float32 [8, 256, 2048], P(None, 'dp', 'tensor')
- moment_output: float32 [8, 256, 2048], P('tensor', 'dp')
- query_weight: bfloat16 [2048, 2048], P(None, 'tensor')
- output_weight: bfloat16 [2048, 2048], P('tensor')
- left_new: float32 [4, 32, 3, 256, 256], P('tensor', 'dp')
- right_new: float32 [4, 32, 3, 256, 256], P('tensor', 'dp')
Inputs may be any that keep to these rules, and one draw needn't show every extreme that they name: `owner`: within one tensor group no device owns more than 3 blocks, and one device owns exactly 3.
All inputs are finite; a program needn't handle non-finite values.
Results may differ from a plain program's by a relative error of at most 0.0004.
Values may be sent and summed in bfloat16 or wider, within the bound.
A program may use at most 192 MiB of HBM per device.

v0:
```python
import jax
import jax.numpy as jnp
from jax import lax
from jax.sharding import PartitionSpec as P

D = 2048
BLK = 256


highest = lax.Precision.HIGHEST
stat_decay = 0.99
moment_decay = 0.9
learn_rate = 0.3
adam_eps = 1e-08
graft_eps = 1e-06


def refresh(blocks, left_stats, right_stats, left_inv, right_inv):
    outer_left = jnp.einsum("cij,ckj->cik", blocks, blocks, precision=highest)
    outer_right = jnp.einsum("cji,cjk->cik", blocks, blocks, precision=highest)
    left_fresh = stat_decay * left_stats + (1.0 - stat_decay) * outer_left
    right_fresh = stat_decay * right_stats + (1.0 - stat_decay) * outer_right
    scaled = jnp.einsum("cij,cjk->cik", left_inv, blocks, precision=highest)
    precond = jnp.einsum("cij,cjk->cik", scaled, right_inv, precision=highest)
    return (left_fresh, right_fresh, precond)


def to_blocks(matrix):
    stacks, height, extent = matrix.shape
    reshaped = matrix.reshape(stacks, height, extent // BLK, BLK).transpose(0, 2, 1, 3)
    return reshaped.reshape(stacks * (extent // BLK), height, BLK)


def from_blocks(blocks, stacks, extent):
    height = blocks.shape[1]
    reshaped = blocks.reshape(stacks, extent // BLK, height, BLK).transpose(0, 2, 1, 3)
    return reshaped.reshape(stacks, height, extent)


def slot_numbers(owner_row):
    total_rows = owner_row.shape[0]
    positions = jnp.arange(total_rows, dtype=jnp.int32)
    same_owner = owner_row[:, None] == owner_row[None, :]
    earlier = positions[None, :] < positions[:, None]
    return jnp.sum((same_owner & earlier).astype(jnp.int32), axis=1)


def on_device(
    grad_query,
    grad_output,
    query_master,
    output_master,
    query_moment,
    output_moment,
    left_stat,
    right_stat,
    left_root,
    right_root,
    owner,
):
    holders = lax.axis_size("dp")
    capacity = left_stat.shape[2]
    height = BLK // holders
    row_blocks = query_master.shape[0]
    slab_width = query_master.shape[2]
    out_blocks = output_master.shape[0]
    full_query = to_blocks(grad_query[0].astype(jnp.float32))
    full_output = to_blocks(grad_output[0].astype(jnp.float32))
    whole_grads = jnp.concatenate([full_query, full_output], axis=0)
    split_at = full_query.shape[0]
    owner_row = owner[0]
    slot_key = owner_row * capacity + slot_numbers(owner_row)
    places = jnp.arange(holders * capacity, dtype=jnp.int32)
    matches = slot_key[None, :] == places[:, None]
    block_ids = jnp.arange(owner_row.shape[0], dtype=jnp.int32)
    source = jnp.sum(jnp.where(matches, block_ids[None, :], 0), axis=1)
    filled = jnp.any(matches, axis=1)
    outgoing = jnp.where(filled[:, None, None], jnp.take(whole_grads, source, axis=0), 0.0)
    owned_blocks = lax.psum_scatter(
        outgoing.reshape(holders, capacity, BLK, BLK), "dp", scatter_dimension=0, tiled=True
    )[0]
    left_fresh, right_fresh, precond = refresh(
        owned_blocks, left_stat[0, 0], right_stat[0, 0], left_root[0, 0], right_root[0, 0]
    )
    back_precond = precond.reshape(capacity, holders, height, BLK).transpose(1, 0, 2, 3)
    back_grads = owned_blocks.reshape(capacity, holders, height, BLK).transpose(1, 0, 2, 3)
    got_precond, got_grads = (
        lax.all_to_all(back_precond, "dp", split_axis=0, concat_axis=0, tiled=True),
        lax.all_to_all(back_grads, "dp", split_axis=0, concat_axis=0, tiled=True),
    )
    grad_pieces = jnp.take(got_grads.reshape(holders * capacity, height, BLK), slot_key, axis=0)
    precond_pieces = jnp.take(
        got_precond.reshape(holders * capacity, height, BLK), slot_key, axis=0
    )
    sum_query = from_blocks(grad_pieces[:split_at], row_blocks, slab_width)
    sum_output = from_blocks(grad_pieces[split_at:], out_blocks, D)
    precond_query = from_blocks(precond_pieces[:split_at], row_blocks, slab_width)
    precond_output = from_blocks(precond_pieces[split_at:], out_blocks, D)
    moment_query = moment_decay * query_moment + (1.0 - moment_decay) * sum_query * sum_query
    moment_output = moment_decay * output_moment + (1.0 - moment_decay) * sum_output * sum_output
    adam_query = sum_query / (jnp.sqrt(moment_query) + adam_eps)
    adam_output = sum_output / (jnp.sqrt(moment_output) + adam_eps)
    adam_local = jnp.stack([jnp.sum(adam_query * adam_query), jnp.sum(adam_output * adam_output)])
    adam_total = lax.psum(adam_local, ("dp", "tensor"))
    position = lax.axis_index("dp")
    mine_source = lax.dynamic_slice_in_dim(source, position * capacity, capacity)
    mine_filled = lax.dynamic_slice_in_dim(filled, position * capacity, capacity)
    slot_squares = jnp.sum(precond * precond, axis=(1, 2))
    is_query = mine_source < split_at
    owned_squares = jnp.stack(
        [
            jnp.sum(jnp.where(mine_filled & is_query, slot_squares, 0.0)),
            jnp.sum(jnp.where(mine_filled & ~is_query, slot_squares, 0.0)),
        ]
    )
    precond_total = lax.psum(owned_squares, ("dp", "tensor"))
    graft_scale = jnp.sqrt(adam_total) / (jnp.sqrt(precond_total) + graft_eps)
    master_query = query_master - learn_rate * graft_scale[0] * precond_query
    master_output = output_master - learn_rate * graft_scale[1] * precond_output
    weights_query, weights_output = (
        lax.all_gather(master_query.astype(jnp.bfloat16), "dp", axis=1, tiled=True),
        lax.all_gather(master_output.astype(jnp.bfloat16), "dp", axis=1, tiled=True),
    )
    query_weight = weights_query.reshape(row_blocks * BLK, slab_width)
    output_weight = weights_output.reshape(out_blocks * BLK, D)
    return (
        master_query,
        master_output,
        moment_query,
        moment_output,
        query_weight,
        output_weight,
        left_fresh[None, None],
        right_fresh[None, None],
    )


def solution(mesh):
    return jax.shard_map(
        on_device,
        mesh=mesh,
        in_specs=(
            P("dp", None, None, "tensor"),
            P("dp", "tensor", None, None),
            P(None, "dp", "tensor"),
            P("tensor", "dp", None),
            P(None, "dp", "tensor"),
            P("tensor", "dp", None),
            P("tensor", "dp", None, None, None),
            P("tensor", "dp", None, None, None),
            P("tensor", "dp", None, None, None),
            P("tensor", "dp", None, None, None),
            P("tensor", None),
        ),
        out_specs=(
            P(None, "dp", "tensor"),
            P("tensor", "dp", None),
            P(None, "dp", "tensor"),
            P("tensor", "dp", None),
            P(None, "tensor"),
            P("tensor", None),
            P("tensor", "dp", None, None, None),
            P("tensor", "dp", None, None, None),
        ),
        check_vma=False,
    )
```

profile of v0, /device:TPU:1, one launch (start us, length us, event | category | flops | bytes accessed | tf_op | source)
XLA Modules:
  0.0 423.1 jit_solution(16131467570751805262)
XLA Ops:
  9.1 2.2 bitcast_convert_fusion
  11.3 2.5 fusion.23
  13.8 2.8 copy.40
  16.6 2.4 convert_bitcast_fusion
  19.0 5.6 %copy.41 = f32[2,8,256,256]{3,2,1,0:T(8,128)} copy(f32[2,8,256,256]{2,3,1,0:T(8,128)} %convert_bitcast_fusion) | data formatting | bytes 8388608 | tf_op jit(solution)/shard_map/reshape | solution.py:31
  24.8 2.1 pad_maximum_fusion.1
  27.6 4.0 pad_maximum_fusion
  31.5 14.4 %gather_fusion = f32[96,256,256]{2,1,0:T(8,128)} fusion(f32[32,256,256]{2,1,0:T(8,128)} %pad_maximum_fusion, s32[1024]{0:T(1024)S(1)} %pad_clamp_fusion.1), kind=kCustom, calls=%fused_computation.2 | custom fusion | bytes 50332032 | tf_op jit(solution)/shard_map/jit(_take)/gather | solution.py:78
  46.0 17.9 %select_select_fusion = f32[32,3,256,256]{3,2,1,0:T(8,128)} fusion(f32[32,3,256,256]{3,2,1,0:T(8,128)} %bitcast.85, pred[32,3]{1,0:T(8,128)(4,1)S(1)} %compare_and_fusion, pred[32,3]{1,0:T(8,128)(4,1)S(1)} %broadcast_in_dim.62), kind=kLoop, calls=%fused_computation.3 | loop fusion | flops 12582912 | bytes 50331840 | tf_op jit(solution)/shard_map/jit(_where)/select_n | solution.py:78
  63.8 143.6 %reduce-scatter.2.cloned.1.call-done = f32[1,3,256,256]{3,2,1,0:T(8,128)} async-done(((f32[32,3,256,256]{3,2,1,0:T(8,128)}), f32[1,3,256,256]{3,2,1,0:T(8,128)}) %reduce-scatter.2.cloned.1.call-update) | async-done | bytes 786448 | tf_op jit(solution)/shard_map/reduce_scatter | solution.py:79
  207.5 2.1 fusion.6
  211.6 5.9 %all-to-all-start.1 = ((f32[32,3,8,256]{3,2,1,0:T(8,128)}), f32[32,3,8,256]{3,2,1,0:T(8,128)S(1)}, u32[]{:S(2)}, u32[]{:S(2)}) async-start(f32[32,3,8,256]{3,2,1,0:T(8,128)} %copy_bitcast_fusion), calls=%async_computation.2 | async-start | bytes 1572864 | tf_op jit(solution)/shard_map/all_to_all | solution.py:88
  218.4 13.3 %all-to-all-done.1 = f32[32,3,8,256]{3,2,1,0:T(8,128)S(1)} async-done(((f32[32,3,8,256]{3,2,1,0:T(8,128)}), f32[32,3,8,256]{3,2,1,0:T(8,128)S(1)}, u32[]{:S(2)}, u32[]{:S(2)}) %all-to-all-start.1) | async-done | bytes 786464 | tf_op jit(solution)/shard_map/all_to_all | solution.py:88
  231.7 4.1 all-to-all-start
  237.2 13.0 %all-to-all-done = f32[32,3,8,256]{3,2,1,0:T(8,128)S(1)} async-done(((f32[32,3,8,256]{3,2,1,0:T(8,128)}), f32[32,3,8,256]{3,2,1,0:T(8,128)S(1)}, u32[]{:S(2)}, u32[]{:S(2)}) %all-to-all-start) | async-done | bytes 786464 | tf_op jit(solution)/shard_map/all_to_all | solution.py:89
  250.9 2.3 multiply_reduce_fusion.2
  253.2 2.2 multiply_reduce_fusion.1
  255.4 2.7 pad_maximum_fusion.2
  258.1 64.3 %all-reduce = (f32[2]{0:T(128)S(1)}, f32[2]{0:T(128)S(1)}) all-reduce(f32[2]{0:T(128)S(1)} %get-tuple-element.36, f32[2]{0:T(128)S(1)} %get-tuple-element.35), channel_id=1, replica_groups=mesh['dp'=32,'tensor'=4] {'dp','tensor'}, use_global_device_ids=true, to_apply=%region_10.12 | all-reduce | flops 4 | bytes 32 | tf_op jit(solution)/shard_map/psum | solution.py:116
  326.9 2.3 fusion.1
  329.2 2.9 fusion.3
  332.2 34.1 %all-gather.3.cloned.1.call-done = bf16[8,256,512]{2,1,0:T(8,128)(2,1)} async-done(((bf16[8,8,512]{2,1,0:T(8,128)(2,1)}), bf16[8,256,512]{2,1,0:T(8,128)(2,1)}) %all-gather.3.cloned.1.call-update) | async-done | bytes 2097168 | tf_op jit(solution)/shard_map/all_gather | solution.py:121
  366.2 45.8 %all-gather.5.cloned.1.call-done = bf16[2,256,2048]{2,1,0:T(8,128)(2,1)} async-done(((bf16[2,8,2048]{2,1,0:T(8,128)(2,1)}), bf16[2,256,2048]{2,1,0:T(8,128)(2,1)}) %all-gather.5.cloned.1.call-update) | async-done | bytes 2097168 | tf_op jit(solution)/shard_map/all_gather | solution.py:122
  412.0 3.2 copy.53
  (49 shorter events, 12.1 us)
Async XLA Ops:
  7.2 202.4 %copy-start = (f32[1,1,3,256,256]{4,3,2,1,0:T(8,128)S(1)}, f32[1,1,3,256,256]{4,3,2,1,0:T(8,128)}, u32[]{:S(2)}) copy-start(f32[1,1,3,256,256]{4,3,2,1,0:T(8,128)} %param.22) | copy-start | bytes 2359300
  7.2 200.3 %reduce-scatter.2.cloned.1.call-start = ((), (), s32[]{:S(2)}) async-start(), calls=%async_computation.3 | async-start | bytes 25952256 | tf_op jit(solution)/shard_map/reduce_scatter | solution.py:79
  19.0 5.7 %copy-start.3 = (f32[8,256,256]{2,1,0:T(8,128)S(1)}, f32[8,256,256]{2,1,0:T(8,128)}, u32[]{:S(2)}) copy-start(f32[8,256,256]{2,1,0:T(8,128)} %get-tuple-element.23) | copy-start | bytes 6291460
  24.7 2.8 copy-start.1
  63.8 143.7 %copy-start.5 = (f32[1,1,3,256,256]{4,3,2,1,0:T(8,128)S(1)}, f32[1,1,3,256,256]{4,3,2,1,0:T(8,128)}, u32[]{:S(2)}) copy-start(f32[1,1,3,256,256]{4,3,2,1,0:T(8,128)} %param.21) | copy-start | bytes 2359300
  207.5 10.0 %copy-start.2 = (f32[1,3,256,256]{3,2,1,0:T(8,128)S(1)}, f32[1,3,256,256]{3,2,1,0:T(8,128)}, u32[]{:S(2)}) copy-start(f32[1,3,256,256]{3,2,1,0:T(8,128)} %reduce-scatter.2.cloned.1.call-done) | copy-start | bytes 2359300
  209.6 26.3 %copy-start.8 = (s32[1,32]{1,0:T(1,128)S(1)}, s32[1,32]{1,0:T(1,128)}, u32[]{:S(2)}) copy-start(s32[1,32]{1,0:T(1,128)} %param.23) | copy-start | bytes 388
  211.6 112.8 %copy-start.7 = (f32[8,8,512]{2,1,0:T(8,128)S(1)}, f32[8,8,512]{2,1,0:T(8,128)}, u32[]{:S(2)}) copy-start(f32[8,8,512]{2,1,0:T(8,128)} %param.15) | copy-start | bytes 393220
  211.6 20.2 %all-to-all-start.1 = ((f32[32,3,8,256]{3,2,1,0:T(8,128)}), f32[32,3,8,256]{3,2,1,0:T(8,128)S(1)}, u32[]{:S(2)}, u32[]{:S(2)}) async-start(f32[32,3,8,256]{3,2,1,0:T(8,128)} %copy_bitcast_fusion), calls=%async_computation.2 | async-start | bytes 1572864 | tf_op jit(solution)/shard_map/all_to_all | solution.py:88
  231.7 18.4 %all-to-all-start = ((f32[32,3,8,256]{3,2,1,0:T(8,128)}), f32[32,3,8,256]{3,2,1,0:T(8,128)S(1)}, u32[]{:S(2)}, u32[]{:S(2)}) async-start(f32[32,3,8,256]{3,2,1,0:T(8,128)} %copy.42), calls=%async_computation.1 | async-start | bytes 1572864 | tf_op jit(solution)/shard_map/all_to_all | solution.py:89
  235.8 130.4 %all-gather.3.cloned.1.call-start = ((), (), s32[]{:S(2)}) async-start(), calls=%async_computation.4 | async-start | bytes 2162688 | tf_op jit(solution)/shard_map/all_gather | solution.py:121
  250.8 76.1 %copy-start.6 = (f32[1,1,3,256,256]{4,3,2,1,0:T(8,128)S(1)}, f32[1,1,3,256,256]{4,3,2,1,0:T(8,128)}, u32[]{:S(2)}) copy-start(f32[1,1,3,256,256]{4,3,2,1,0:T(8,128)} %param.20) | copy-start | bytes 2359300
  325.1 87.0 %all-gather.5.cloned.1.call-start = ((), (), s32[]{:S(2)}) async-start(), calls=%async_computation.5 | async-start | bytes 2162688 | tf_op jit(solution)/shard_map/all_gather | solution.py:122
  412.0 3.2 copy-start.4
Sparse Core Ops, SparseCore 0:
  64.0 143.4 reduce-scatter.1
  325.2 40.9 all-gather.2
  369.1 42.8 all-gather.4
where the time goes:
time: 424 us; the launch traced here: 423 us
  waiting for transfers between devices  250 us (59%)
  blocking collectives  64.3 us (15%)
  other arithmetic  40.6 us (10%)
  local copies, waits for them, and re-layouts  34.4 us (8%)
  between operations  15.3 us (4%)
  starting transfers between devices  10.3 us (2%)
  matrix products  8.34 us (2%)
    reduce_scatter x1, waiting for transfers between devices, on_device(): lax.psum_scatter(outgoing.reshape(holders, capacity, BLK, BLK), 'dp', sca...  144 us
    psum x1, blocking collectives, on_device(): precond_total = lax.psum(owned_squares, ('dp', 'tensor'))  64.3 us
    all_gather x1, waiting for transfers between devices, on_device(): lax.all_gather(master_output.astype(jnp.bfloat16), 'dp', axis=1, tiled=True)  45.8 us
    all_gather x1, waiting for transfers between devices, on_device(): lax.all_gather(master_query.astype(jnp.bfloat16), 'dp', axis=1, tiled=True)  34.1 us
    select_n x1, other arithmetic, on_device(): jnp.where(filled[:, None, None], jnp.take(whole_grads, source, axis=0), 0.0)  17.9 us
    gather x1, local copies, waits for them, and re-layouts, on_device(): jnp.take(whole_grads, source, axis=0)  14.4 us
    all_to_all x1, waiting for transfers between devices, on_device(): lax.all_to_all(back_precond, 'dp', split_axis=0, concat_axis=0, tiled=True)  13.3 us
    all_to_all x1, waiting for transfers between devices, on_device(): lax.all_to_all(back_grads, 'dp', split_axis=0, concat_axis=0, tiled=True)  13 us
  transfers between devices with their start and end apart: 5, of which 5 were waited for; matrix products, arithmetic and copies ran while one was open for 2% of the time, Pallas kernels for 0%

commit v1 on v0

v1 whole, which is shorter than its diff:
```python
import functools

import jax
import jax.numpy as jnp
from jax import lax
from jax.experimental import pallas as pl
from jax.experimental.pallas import tpu as pltpu
from jax.sharding import PartitionSpec as P

BLK = 256
N = 32
GROUPS = 4
CAP = 3
NB = 32
QB = 16
HEIGHT = BLK // N

highest = lax.Precision.HIGHEST
stat_decay = 0.99
moment_decay = 0.9
learn_rate = 0.3
adam_eps = 1e-08
graft_eps = 1e-06

MESH = pl.DeviceIdType.MESH


def tables(owner_row):
    ids = jnp.arange(NB, dtype=jnp.int32)
    same = owner_row[:, None] == owner_row[None, :]
    slot = jnp.sum((same & (ids[None, :] < ids[:, None])).astype(jnp.int32), axis=1)
    key = owner_row * CAP + slot
    places = jnp.arange(N * CAP, dtype=jnp.int32)
    source = NB + jnp.sum(jnp.where(key[None, :] == places[:, None], ids[None, :] - NB, 0), axis=1)
    return source, key


def kernel(
    source, key, gq, go, qmast, omast, qmom, omom, lstat, rstat, lroot, rroot,
    mq_out, mo_out, vq_out, vo_out, wq_out, wo_out, ln_out, rn_out,
    rq, ro, sq, so, blocks, gsend, gfull, pbuf, prec,
    qm, om, qv, ov, ls, rs, lr, rr, wq, wo,
    znorm, znet, nsend, nnet,
    in_sem, out_sem, rs_sq, rs_so, rs_rq, rs_ro, g_s, g_r, p_s, p_r, z_s, z_r, n_s, n_r, w_sq, w_so, w_rq, w_ro,
):
    me = lax.axis_index("dp")
    z = lax.axis_index("tensor")

    def peer(k):
        return lax.rem(me + k, N)

    loads = [
        pltpu.make_async_copy(src, dst, in_sem.at[i])
        for i, (src, dst) in enumerate(
            [(lroot, lr), (rroot, rr), (qmom, qv), (omom, ov), (qmast, qm), (omast, om), (lstat, ls), (rstat, rs)]
        )
    ]
    for copy in loads:
        copy.start()

    barrier = pltpu.get_barrier_semaphore()

    def greet(k, _):
        pl.semaphore_signal(barrier, inc=1, device_id={"dp": peer(k)}, device_id_type=MESH)
        return 0

    lax.fori_loop(1, N, greet, 0)
    for j in range(1, GROUPS):
        pl.semaphore_signal(
            barrier, inc=1, device_id={"tensor": lax.rem(z + j, GROUPS)}, device_id_type=MESH
        )
    pl.semaphore_wait(barrier, N - 1 + GROUPS - 1)

    def rows(d):
        return pl.ds(pl.multiple_of(d * HEIGHT, HEIGHT), HEIGHT)

    def grad_copies(to, slot):
        return (
            pltpu.make_async_remote_copy(
                gq.at[0, :, rows(to), :], rq.at[slot], rs_sq.at[to], rs_rq.at[slot],
                device_id={"dp": to}, device_id_type=MESH,
            ),
            pltpu.make_async_remote_copy(
                go.at[0, :, rows(to), :], ro.at[slot], rs_so.at[to], rs_ro.at[slot],
                device_id={"dp": to}, device_id_type=MESH,
            ),
        )

    def send_grads(k, _):
        for copy in grad_copies(peer(k), me):
            copy.start()
        return 0

    lax.fori_loop(1, N, send_grads, 0)
    own_q = pltpu.make_async_copy(gq.at[0, :, rows(me), :], rq.at[me], rs_rq.at[me])
    own_o = pltpu.make_async_copy(go.at[0, :, rows(me), :], ro.at[me], rs_ro.at[me])
    own_q.start()
    own_o.start()
    own_q.wait()
    own_o.wait()
    sq[...] = rq[me].astype(jnp.float32)
    so[...] = ro[me].astype(jnp.float32)

    def add_grads(k, _):
        frm = peer(k)
        for copy in grad_copies(frm, frm):
            copy.wait_recv()
        sq[...] += rq[frm].astype(jnp.float32)
        so[...] += ro[frm].astype(jnp.float32)
        return 0

    lax.fori_loop(1, N, add_grads, 0)

    for r in range(8):
        for c in range(2):
            blocks[r * 2 + c] = sq[r, :, c * BLK : (c + 1) * BLK]
    for r in range(2):
        for c in range(8):
            blocks[QB + r * 8 + c] = so[r, :, c * BLK : (c + 1) * BLK]
    blocks[NB] = jnp.zeros((HEIGHT, BLK), jnp.float32)

    def place(d, _):
        for s in range(CAP):
            gsend[d, s] = blocks[source[d * CAP + s]]
        return 0

    lax.fori_loop(0, N, place, 0)

    def g_copy(to, slot):
        return pltpu.make_async_remote_copy(
            gsend.at[to], gfull.at[:, rows(slot), :], g_s.at[to], g_r.at[slot],
            device_id={"dp": to}, device_id_type=MESH,
        )

    def send_blocks(k, _):
        g_copy(peer(k), me).start()
        return 0

    lax.fori_loop(1, N, send_blocks, 0)
    own_g = pltpu.make_async_copy(gsend.at[me], gfull.at[:, rows(me), :], g_r.at[me])
    own_g.start()

    loads[2].wait()
    loads[3].wait()
    fresh_q = moment_decay * qv[...] + (1.0 - moment_decay) * sq[...] * sq[...]
    qv[...] = fresh_q
    fresh_o = moment_decay * ov[...] + (1.0 - moment_decay) * so[...] * so[...]
    ov[...] = fresh_o
    adam_q = sq[...] / (jnp.sqrt(fresh_q) + adam_eps)
    adam_o = so[...] / (jnp.sqrt(fresh_o) + adam_eps)
    adam_q2 = jnp.sum(adam_q * adam_q)
    adam_o2 = jnp.sum(adam_o * adam_o)
    stores = [
        pltpu.make_async_copy(qv, vq_out, out_sem.at[0]),
        pltpu.make_async_copy(ov, vo_out, out_sem.at[1]),
    ]
    for copy in stores:
        copy.start()

    own_g.wait()

    def wait_blocks(k, _):
        frm = peer(k)
        g_copy(frm, frm).wait_recv()
        return 0

    lax.fori_loop(1, N, wait_blocks, 0)

    loads[0].wait()
    loads[1].wait()

    def dot(a, b, dims=((1,), (0,))):
        return lax.dot_general(a, b, (dims, ((), ())), precision=highest, preferred_element_type=jnp.float32)

    prec_q2 = 0.0
    prec_o2 = 0.0
    for s in range(CAP):
        pre = dot(dot(lr[s], gfull[s]), rr[s])
        pbuf[s] = pre
        square = jnp.sum(pre * pre)
        is_query = source[me * CAP + s] < QB
        prec_q2 = prec_q2 + jnp.where(is_query, square, 0.0)
        prec_o2 = prec_o2 + jnp.where(is_query, 0.0, square)

    def p_copy(to, slot):
        return pltpu.make_async_remote_copy(
            pbuf.at[:, rows(to), :], prec.at[pl.ds(slot * CAP, CAP)], p_s.at[to], p_r.at[slot],
            device_id={"dp": to}, device_id_type=MESH,
        )

    def send_prec(k, _):
        p_copy(peer(k), me).start()
        return 0

    lax.fori_loop(1, N, send_prec, 0)
    own_p = pltpu.make_async_copy(pbuf.at[:, rows(me), :], prec.at[pl.ds(me * CAP, CAP)], p_r.at[me])
    own_p.start()

    lane = lax.broadcasted_iota(jnp.int32, (8, 128), 1)
    mine = jnp.where(lane == 0, adam_q2, jnp.where(lane == 1, adam_o2, jnp.where(lane == 2, prec_q2, prec_o2)))
    znorm[...] = mine

    def z_copy(to, slot):
        return pltpu.make_async_remote_copy(
            znorm, znet.at[slot], z_s.at[to], z_r.at[slot], device_id={"tensor": to}, device_id_type=MESH
        )

    for j in range(1, GROUPS):
        z_copy(lax.rem(z + j, GROUPS), z).start()

    loads[6].wait()
    loads[7].wait()
    znet[z] = mine
    for j in range(1, GROUPS):
        frm = lax.rem(z + j, GROUPS)
        z_copy(frm, frm).wait_recv()
    total = znet[0] + znet[1] + znet[2] + znet[3]
    nsend[...] = total

    def n_copy(to, slot):
        return pltpu.make_async_remote_copy(
            nsend, nnet.at[slot], n_s.at[to], n_r.at[slot], device_id={"dp": to}, device_id_type=MESH
        )

    def send_norm(k, _):
        n_copy(peer(k), me).start()
        return 0

    lax.fori_loop(1, N, send_norm, 0)
    nnet[me] = total

    for s in range(CAP):
        g = gfull[s]
        ls[s] = stat_decay * ls[s] + (1.0 - stat_decay) * dot(g, g, ((1,), (1,)))
        rs[s] = stat_decay * rs[s] + (1.0 - stat_decay) * dot(g, g, ((0,), (0,)))
    stores += [
        pltpu.make_async_copy(ls, ln_out, out_sem.at[2]),
        pltpu.make_async_copy(rs, rn_out, out_sem.at[3]),
    ]
    stores[2].start()
    stores[3].start()

    own_p.wait()

    def wait_prec(k, _):
        frm = peer(k)
        p_copy(frm, frm).wait_recv()
        n_copy(frm, frm).wait_recv()
        return 0

    lax.fori_loop(1, N, wait_prec, 0)
    norms = jnp.sum(nnet[...], axis=0)

    def pick(i):
        return jnp.sum(jnp.where(lane == i, norms, 0.0), axis=1, keepdims=True)[0:1]

    scale_q = learn_rate * (jnp.sqrt(pick(0)) / (jnp.sqrt(pick(2)) + graft_eps))
    scale_o = learn_rate * (jnp.sqrt(pick(1)) / (jnp.sqrt(pick(3)) + graft_eps))

    loads[4].wait()
    loads[5].wait()
    for r in range(8):
        for c in range(2):
            cols = slice(c * BLK, (c + 1) * BLK)
            fresh = qm[r, :, cols] - scale_q * prec[key[r * 2 + c]]
            qm[r, :, cols] = fresh
            wq[r, :, cols] = fresh.astype(jnp.bfloat16)
    for r in range(2):
        for c in range(8):
            cols = slice(c * BLK, (c + 1) * BLK)
            fresh = om[r, :, cols] - scale_o * prec[key[QB + r * 8 + c]]
            om[r, :, cols] = fresh
            wo[r, :, cols] = fresh.astype(jnp.bfloat16)

    def w_copies(to, slot):
        return (
            pltpu.make_async_remote_copy(
                wq, wq_out.at[:, rows(slot), :], w_sq.at[to], w_rq.at[slot],
                device_id={"dp": to}, device_id_type=MESH,
            ),
            pltpu.make_async_remote_copy(
                wo, wo_out.at[:, rows(slot), :], w_so.at[to], w_ro.at[slot],
                device_id={"dp": to}, device_id_type=MESH,
            ),
        )

    def send_weights(k, _):
        for copy in w_copies(peer(k), me):
            copy.start()
        return 0

    lax.fori_loop(1, N, send_weights, 0)
    stores += [
        pltpu.make_async_copy(qm, mq_out, out_sem.at[4]),
        pltpu.make_async_copy(om, mo_out, out_sem.at[5]),
        pltpu.make_async_copy(wq, wq_out.at[:, rows(me), :], out_sem.at[6]),
        pltpu.make_async_copy(wo, wo_out.at[:, rows(me), :], out_sem.at[7]),
    ]
    for copy in stores[4:]:
        copy.start()

    def finish(k, _):
        d = peer(k)
        for copy in w_copies(d, d):
            copy.wait_recv()
            copy.wait_send()
        for copy in grad_copies(d, me):
            copy.wait_send()
        g_copy(d, me).wait_send()
        p_copy(d, me).wait_send()
        n_copy(d, me).wait_send()
        return 0

    lax.fori_loop(1, N, finish, 0)
    for j in range(1, GROUPS):
        z_copy(lax.rem(z + j, GROUPS), z).wait_send()
    for copy in stores:
        copy.wait()


def on_device(
    grad_query, grad_output, query_master, output_master, query_moment, output_moment,
    left_stat, right_stat, left_root, right_root, owner,
):
    source, key = tables(owner[0])
    f32, bf16 = jnp.float32, jnp.bfloat16
    stat = (CAP, BLK, BLK)
    qpiece, opiece = query_master.shape, output_master.shape
    anywhere = pl.BlockSpec(memory_space=pl.ANY)
    scalars = pl.BlockSpec(memory_space=pltpu.SMEM)
    dma = pltpu.SemaphoreType.DMA
    outs = pl.pallas_call(
        kernel,
        out_shape=[
            jax.ShapeDtypeStruct(qpiece, f32),
            jax.ShapeDtypeStruct(opiece, f32),
            jax.ShapeDtypeStruct(qpiece, f32),
            jax.ShapeDtypeStruct(opiece, f32),
            jax.ShapeDtypeStruct((8, BLK, 512), bf16),
            jax.ShapeDtypeStruct((2, BLK, 2048), bf16),
            jax.ShapeDtypeStruct(stat, f32),
            jax.ShapeDtypeStruct(stat, f32),
        ],
        in_specs=[scalars, scalars] + [anywhere] * 10,
        out_specs=[anywhere] * 8,
        scratch_shapes=[
            pltpu.VMEM((N,) + qpiece, bf16),
            pltpu.VMEM((N,) + opiece, bf16),
            pltpu.VMEM(qpiece, f32),
            pltpu.VMEM(opiece, f32),
            pltpu.VMEM((NB + 1, HEIGHT, BLK), f32),
            pltpu.VMEM((N, CAP, HEIGHT, BLK), f32),
            pltpu.VMEM(stat, f32),
            pltpu.VMEM(stat, f32),
            pltpu.VMEM((N * CAP, HEIGHT, BLK), f32),
            pltpu.VMEM(qpiece, f32),
            pltpu.VMEM(opiece, f32),
            pltpu.VMEM(qpiece, f32),
            pltpu.VMEM(opiece, f32),
            pltpu.VMEM(stat, f32),
            pltpu.VMEM(stat, f32),
            pltpu.VMEM(stat, f32),
            pltpu.VMEM(stat, f32),
            pltpu.VMEM(qpiece, bf16),
            pltpu.VMEM(opiece, bf16),
            pltpu.VMEM((8, 128), f32),
            pltpu.VMEM((GROUPS, 8, 128), f32),
            pltpu.VMEM((8, 128), f32),
            pltpu.VMEM((N, 8, 128), f32),
            dma((8,)),
            dma((8,)),
        ]
        + [dma((N,))] * 8
        + [dma((GROUPS,))] * 2
        + [dma((N,))] * 6,
        compiler_params=pltpu.CompilerParams(collective_id=0, has_side_effects=True, vmem_limit_bytes=60 << 20),
        name="shampoo",
    )(
        source, key, grad_query, grad_output, query_master, output_master, query_moment, output_moment,
        left_stat[0, 0], right_stat[0, 0], left_root[0, 0], right_root[0, 0],
    )
    mq, mo, vq, vo, wq, wo, ln, rn = outs
    return mq, mo, vq, vo, wq.reshape(-1, 512), wo.reshape(-1, 2048), ln[None, None], rn[None, None]


def solution(mesh):
    return jax.shard_map(
        on_device,
        mesh=mesh,
        in_specs=(
            P("dp", None, None, "tensor"),
            P("dp", "tensor", None, None),
            P(None, "dp", "tensor"),
            P("tensor", "dp", None),
            P(None, "dp", "tensor"),
            P("tensor", "dp", None),
            P("tensor", "dp", None, None, None),
            P("tensor", "dp", None, None, None),
            P("tensor", "dp", None, None, None),
            P("tensor", "dp", None, None, None),
            P("tensor", None),
        ),
        out_specs=(
            P(None, "dp", "tensor"),
            P("tensor", "dp", None),
            P(None, "dp", "tensor"),
            P("tensor", "dp", None),
            P(None, "tensor"),
            P("tensor", None),
            P("tensor", "dp", None, None, None),
            P("tensor", "dp", None, None, None),
        ),
        check_vma=False,
    )
```

time: 424 us -> 198 us (0.47)
  waiting for transfers between devices: 250 us -> 0 us
  Pallas kernels: 0 us -> 181 us
  blocking collectives: 64.3 us -> 0 us
  other arithmetic: 40.6 us -> 3.35 us
  local copies, waits for them, and re-layouts: 34.4 us -> 12.9 us
  between operations: 15.3 us -> 0.65 us
  starting transfers between devices: 10.3 us -> 0 us
  matrix products: 8.34 us -> 0 us
    pallas_call x0 -> x1, Pallas kernels: none -> 181 us  [on_device(): pl.pallas_call(kernel, out_shape=[jax.ShapeDtypeStruct(qpiece, f32), jax....]
    reduce_scatter x1 -> x0, waiting for transfers between devices: 144 us -> none  [on_device(): lax.psum_scatter(outgoing.reshape(holders, capacity, BLK, BLK), 'dp', sca...]
    all_gather x2 -> x0, waiting for transfers between devices: 79.9 us -> none  [the longest x1 45.8 us: on_device(): lax.all_gather(master_output.astype(jnp.bfloat16), 'dp', axis=1, tiled=True)]
    psum x1 -> x0, blocking collectives: 64.3 us -> none  [on_device(): precond_total = lax.psum(owned_squares, ('dp', 'tensor'))]
    all_to_all x2 -> x0, waiting for transfers between devices: 26.3 us -> none  [the longest x1 13.3 us: on_device(): lax.all_to_all(back_precond, 'dp', split_axis=0, concat_axis=0, tiled=True)]
    select_n x3 -> x0, other arithmetic: 18 us -> none  [the longest x1 17.9 us: on_device(): jnp.where(filled[:, None, None], jnp.take(whole_grads, source, axis=0), 0.0)]
    gather x3 -> x0, local copies, waits for them, and re-layouts: 15.6 us -> none  [the longest x1 14.4 us: on_device(): jnp.take(whole_grads, source, axis=0)]
    all_to_all x2 -> x0, starting transfers between devices: 10 us -> none  [the longest x1 5.93 us: on_device(): lax.all_to_all(back_precond, 'dp', split_axis=0, concat_axis=0, tiled=True)]
  transfers between devices with their start and end apart: 5 -> 0, of which waited for: 5 -> 0; matrix products, arithmetic and copies ran while one was open for 2% -> 0% of each run, Pallas kernels for 0% -> 0%
where the time goes in v1:
time: 198 us
  Pallas kernels  181 us (91%)
  local copies, waits for them, and re-layouts  12.9 us (7%)
  other arithmetic  3.35 us (2%)
    pallas_call x1, Pallas kernels, on_device(): pl.pallas_call(kernel, out_shape=[jax.ShapeDtypeStruct(qpiece, f32), jax....  181 us
    unnamed x14, local copies, waits for them, and re-layouts  12.9 us

profile of v1, /device:TPU:1, one launch (start us, length us, event | category | flops | bytes accessed | tf_op | source)
XLA Modules:
  0.0 198.1 jit_solution(11698491253855143213)
XLA Ops:
  0.6 0.9 convert_reduce_fusion
  1.5 1.2 multiply_add_fusion.key
  2.7 0.7 fusion.1
  3.4 0.1 select_reduce_fusion
  3.5 0.5 broadcast_add_fusion.source
  4.0 181.2 %shampoo.1 = (f32[8,8,512]{2,1,0:T(8,128)}, f32[2,8,2048]{2,1,0:T(8,128)}, f32[8,8,512]{2,1,0:T(8,128)}, f32[2,8,2048]{2,1,0:T(8,128)}, bf16[8,256,512]{2,1,0:T(...) custom-call(s32[96]{0:T(128)} %broadcast_add_fusion.source, ...), custom_call_target="tpu_custom_call" | custom-call | tf_op jit(solution)/shard_map/shampoo/pallas_call | solution.py:332
  185.2 1.6 copy.27
  186.8 1.6 copy.28
  188.3 1.6 copy.29
  189.9 1.6 copy.30
  191.5 0.0 copy-start
  191.5 3.2 %copy.31 = bf16[2048,512]{1,0:T(8,128)(2,1)} copy(bf16[2048,512]{1,0:T(8,128)(2,1)} %bitcast.17) | data formatting | bytes 4194304
  194.7 0.0 copy-done
  194.7 0.0 copy-start.2
  194.7 0.0 copy-start.1
  194.7 1.3 copy.32
  196.0 0.4 copy-done.2
  196.3 0.9 copy.33
  197.2 0.0 copy-done.1
  197.2 0.9 copy.34
  (1 shorter events, 0.0 us)
Async XLA Ops:
  191.5 3.2 %copy-start = (bf16[2,256,2048]{2,1,0:T(8,128)(2,1)S(1)}, bf16[2,256,2048]{2,1,0:T(8,128)(2,1)}, u32[]{:S(2)}) copy-start(bf16[2,256,2048]{2,1,0:T(8,128)(2,1)} %get-tuple-element.21) | copy-start | bytes 6291460
  194.7 1.7 copy-start.2
  194.7 2.6 %copy-start.1 = (f32[3,256,256]{2,1,0:T(8,128)S(1)}, f32[3,256,256]{2,1,0:T(8,128)}, u32[]{:S(2)}) copy-start(f32[3,256,256]{2,1,0:T(8,128)} %get-tuple-element.23) | copy-start | bytes 2359300

commit v2 on v1

--- a/solution.py
+++ b/solution.py
@@ -14,6 +14,7 @@
 NB = 32
 QB = 16
 HEIGHT = BLK // N
+LIMIT = 36
 
 highest = lax.Precision.HIGHEST
 stat_decay = 0.99
@@ -35,20 +36,79 @@
     return source, key
 
 
+SIDE = 4
+
+
+class Grads:
+    def __init__(self, query, raw, refs, sems):
+        self.query, self.raw = query, raw
+        self.own, self.other, self.s1, self.rl1, self.rx1, self.t, self.rl2, self.rx2, self.total = refs
+        self.sems = sems
+
+    def at(self, ref, f, s=slice(None), r=slice(None)):
+        return ref.at[r, s, f] if self.query else ref.at[r, f, s]
+
+
+def halves(ref):
+    rows = ref.shape[0]
+    return pl.ds(0, rows // 2), pl.ds(rows // 2, rows // 2)
+
+
 def kernel(
     source, key, gq, go, qmast, omast, qmom, omom, lstat, rstat, lroot, rroot,
     mq_out, mo_out, vq_out, vo_out, wq_out, wo_out, ln_out, rn_out,
-    rq, ro, sq, so, blocks, gsend, gfull, pbuf, prec,
+    q_own, q_oth, q_s1, q_rl1, q_rx1, q_t, q_rl2, q_rx2, sq,
+    o_own, o_oth, o_s1, o_rl1, o_rx1, o_t, o_rl2, o_rx2, so,
+    blocks, gsend, gfull, pbuf, prec,
     qm, om, qv, ov, ls, rs, lr, rr, wq, wo,
     znorm, znet, nsend, nnet,
-    in_sem, out_sem, rs_sq, rs_so, rs_rq, rs_ro, g_s, g_r, p_s, p_r, z_s, z_r, n_s, n_r, w_sq, w_so, w_rq, w_ro,
+    in_sem, out_sem, own_sem, pair_s, pair_r, one_s, one_r, two_s, two_r,
+    g_s, g_r, p_s, p_r, z_s, z_r, n_s, n_r, w_s, w_r, x_s, x_r,
 ):
     me = lax.axis_index("dp")
     z = lax.axis_index("tensor")
+    core = lax.rem(me, 2)
+    col = lax.rem(me // 2, SIDE)
+    row = me // (2 * SIDE)
+    other = 1 - core
 
     def peer(k):
         return lax.rem(me + k, N)
 
+    def device(y, x, c):
+        return {"dp": (y * SIDE + x) * 2 + c}
+
+    def turn(i, k):
+        return lax.rem(i + k + SIDE, SIDE)
+
+    partner = device(row, col, other)
+    east, west = device(row, turn(col, 1), core), device(row, turn(col, -1), core)
+    south, north = device(turn(row, 1), col, core), device(turn(row, -1), col, core)
+
+    def remote(src, dst, send, recv, to):
+        return pltpu.make_async_remote_copy(src, dst, send, recv, device_id=to, device_id_type=MESH)
+
+    Q = Grads(True, gq, (q_own, q_oth, q_s1, q_rl1, q_rx1, q_t, q_rl2, q_rx2, sq), 0)
+    O = Grads(False, go, (o_own, o_oth, o_s1, o_rl1, o_rx1, o_t, o_rl2, o_rx2, so), 1)
+    Q.f, Q.s, O.f, O.s = col, row, row, col
+    Q.plus, Q.minus, Q.up, Q.down = east, west, south, north
+    O.plus, O.minus, O.up, O.down = south, north, east, west
+    both = (Q, O)
+    order = (2, 1, 3, 0)
+
+    def raw_chunk(a, k, c):
+        f = turn(a.f, k)
+        if a.query:
+            return a.raw.at[0, :, :, f, c]
+        return a.raw.at[0, :, f, :, c]
+
+    own_loads = {}
+    for k in order:
+        for a in both:
+            own_loads[a.sems, k] = pltpu.make_async_copy(
+                raw_chunk(a, k, core), a.own.at[k], own_sem.at[a.sems, k]
+            )
+            own_loads[a.sems, k].start()
     loads = [
         pltpu.make_async_copy(src, dst, in_sem.at[i])
         for i, (src, dst) in enumerate(
@@ -71,45 +131,96 @@
         )
     pl.semaphore_wait(barrier, N - 1 + GROUPS - 1)
 
+    sent = []
+
+    def launch(copy):
+        copy.start()
+        sent.append(copy)
+        return copy
+
+    pairs = {}
+    for k in order:
+        for a in both:
+            pairs[a.sems, k] = launch(
+                remote(raw_chunk(a, k, other), a.other.at[k], pair_s.at[a.sems, k], pair_r.at[a.sems, k], partner)
+            )
+
+    def pair_sum(a, k):
+        own_loads[a.sems, k].wait()
+        pairs[a.sems, k].wait_recv()
+        a.s1[k] = a.own[k].astype(jnp.float32) + a.other[k].astype(jnp.float32)
+
+    def chunk_copies(a, send, recv, piece, rl, rx, plus, minus):
+        lo, hi = halves(rx.at[0])
+        return dict(
+            relay_plus=remote(piece(2, lo), rl.at[0], send.at[0], recv.at[0], plus),
+            relay_minus=remote(piece(2, hi), rl.at[1], send.at[1], recv.at[1], minus),
+            near_plus=remote(piece(1, hi), rx.at[0, hi], send.at[2], recv.at[2], plus),
+            near_minus=remote(piece(3, lo), rx.at[1, lo], send.at[3], recv.at[3], minus),
+            last_plus=remote(piece(1, lo), rx.at[0, lo], send.at[4], recv.at[4], plus),
+            last_minus=remote(piece(3, hi), rx.at[1, hi], send.at[5], recv.at[5], minus),
+        )
+
+    one, two = {}, {}
+    for a in both:
+        i = a.sems
+        one[i] = chunk_copies(
+            a, one_s.at[i], one_r.at[i], lambda k, r, a=a: a.s1.at[k, r], a.rl1, a.rx1, a.plus, a.minus
+        )
+        two[i] = chunk_copies(
+            a, two_s.at[i], two_r.at[i], lambda k, r, a=a: a.t.at[turn(a.s, k), r], a.rl2, a.rx2, a.up, a.down
+        )
+
+    for a in both:
+        pair_sum(a, 2)
+        launch(one[a.sems]["relay_plus"])
+        launch(one[a.sems]["relay_minus"])
+    for a in both:
+        pair_sum(a, 1)
+        launch(one[a.sems]["near_plus"])
+    for a in both:
+        pair_sum(a, 3)
+        launch(one[a.sems]["near_minus"])
+    for a in both:
+        pair_sum(a, 0)
+    for a in both:
+        lo, hi = halves(a.s1.at[0])
+        one[a.sems]["relay_plus"].wait_recv()
+        a.s1[1, lo] += a.rl1[0]
+        launch(one[a.sems]["last_plus"])
+        one[a.sems]["relay_minus"].wait_recv()
+        a.s1[3, hi] += a.rl1[1]
+        launch(one[a.sems]["last_minus"])
+    for a in both:
+        for name in ("near_plus", "near_minus", "last_plus", "last_minus"):
+            one[a.sems][name].wait_recv()
+        for k in (2, 1, 3, 0):
+            s = turn(a.s, k)
+            a.t[s] = a.s1[0, :, s] + a.rx1[0, :, s] + a.rx1[1, :, s]
+            if k == 2:
+                launch(two[a.sems]["relay_plus"])
+                launch(two[a.sems]["relay_minus"])
+            elif k == 1:
+                launch(two[a.sems]["near_plus"])
+            elif k == 3:
+                launch(two[a.sems]["near_minus"])
+    for a in both:
+        lo, hi = halves(a.t.at[0])
+        s = turn(a.s, 1)
+        two[a.sems]["relay_plus"].wait_recv()
+        a.t[s, lo] += a.rl2[0]
+        launch(two[a.sems]["last_plus"])
+        s = turn(a.s, 3)
+        two[a.sems]["relay_minus"].wait_recv()
+        a.t[s, hi] += a.rl2[1]
+        launch(two[a.sems]["last_minus"])
+    for a in both:
+        for name in ("near_plus", "near_minus", "last_plus", "last_minus"):
+            two[a.sems][name].wait_recv()
+        a.total[...] = a.t[a.s] + a.rx2[0] + a.rx2[1]
+
     def rows(d):
         return pl.ds(pl.multiple_of(d * HEIGHT, HEIGHT), HEIGHT)
-
-    def grad_copies(to, slot):
-        return (
-            pltpu.make_async_remote_copy(
-                gq.at[0, :, rows(to), :], rq.at[slot], rs_sq.at[to], rs_rq.at[slot],
-                device_id={"dp": to}, device_id_type=MESH,
-            ),
-            pltpu.make_async_remote_copy(
-                go.at[0, :, rows(to), :], ro.at[slot], rs_so.at[to], rs_ro.at[slot],
-                device_id={"dp": to}, device_id_type=MESH,
-            ),
-        )
-
-    def send_grads(k, _):
-        for copy in grad_copies(peer(k), me):
-            copy.start()
-        return 0
-
-    lax.fori_loop(1, N, send_grads, 0)
-    own_q = pltpu.make_async_copy(gq.at[0, :, rows(me), :], rq.at[me], rs_rq.at[me])
-    own_o = pltpu.make_async_copy(go.at[0, :, rows(me), :], ro.at[me], rs_ro.at[me])
-    own_q.start()
-    own_o.start()
-    own_q.wait()
-    own_o.wait()
-    sq[...] = rq[me].astype(jnp.float32)
-    so[...] = ro[me].astype(jnp.float32)
-
-    def add_grads(k, _):
-        frm = peer(k)
-        for copy in grad_copies(frm, frm):
-            copy.wait_recv()
-        sq[...] += rq[frm].astype(jnp.float32)
-        so[...] += ro[frm].astype(jnp.float32)
-        return 0
-
-    lax.fori_loop(1, N, add_grads, 0)
 
     for r in range(8):
         for c in range(2):
@@ -272,40 +383,105 @@
             om[r, :, cols] = fresh
             wo[r, :, cols] = fresh.astype(jnp.bfloat16)
 
-    def w_copies(to, slot):
-        return (
-            pltpu.make_async_remote_copy(
-                wq, wq_out.at[:, rows(slot), :], w_sq.at[to], w_rq.at[slot],
-                device_id={"dp": to}, device_id_type=MESH,
-            ),
-            pltpu.make_async_remote_copy(
-                wo, wo_out.at[:, rows(slot), :], w_so.at[to], w_ro.at[slot],
-                device_id={"dp": to}, device_id_type=MESH,
-            ),
-        )
-
-    def send_weights(k, _):
-        for copy in w_copies(peer(k), me):
-            copy.start()
-        return 0
-
-    lax.fori_loop(1, N, send_weights, 0)
+    class Gather:
+        pass
+
+    GQ, GO = Gather(), Gather()
+    for g, a, src, dst in ((GQ, Q, wq, wq_out), (GO, O, wo, wo_out)):
+        g.a, g.src, g.dst, g.i = a, src, dst, a.sems
+
+    def place_of(g, p, q, r=slice(None), c=None):
+        f, s = turn(g.a.f, p), turn(g.a.s, q)
+        y, x = (s, f) if g.a.query else (f, s)
+        return g.dst.at[r, y * SIDE + x, core if c is None else c]
+
+    def move(g, n, p, q, to, r=slice(None), fresh=False):
+        src = g.src.at[r] if fresh else place_of(g, p, q, r)
+        return remote(src, place_of(g, p, q, r), w_s.at[g.i, n], w_r.at[g.i, n], to)
+
+    def incoming(g, n, p, q, r=slice(None)):
+        there = place_of(g, p, q, r)
+        remote(there, there, w_s.at[g.i, n], w_r.at[g.i, n], partner).wait_recv()
+
+    def number(p, q):
+        return (p % SIDE) * SIDE + q % SIDE
+
+    def share(g, p, q, fresh=False):
+        src = g.src if fresh else place_of(g, p, q)
+        n = number(p, q)
+        launch(remote(src, place_of(g, p, q), x_s.at[g.i, n], x_r.at[g.i, n], partner))
+
+    gathers = (GQ, GO)
+
+    def spread(g, p, fresh=False):
+        base = 4 + 4 * (p % SIDE)
+        launch(move(g, base + 0, p, 0, g.a.up, fresh=fresh))
+        launch(move(g, base + 1, p, 0, g.a.down, fresh=fresh))
+
+    def relay(g, p):
+        base = 4 + 4 * (p % SIDE)
+        lo, hi = halves(g.src)
+        incoming(g, base + 0, p, -1)
+        launch(move(g, base + 2, p, -1, g.a.up, lo))
+        share(g, p, -1)
+        incoming(g, base + 1, p, 1)
+        launch(move(g, base + 3, p, 1, g.a.down, hi))
+        share(g, p, 1)
+
+    def far(g, p):
+        base = 4 + 4 * (p % SIDE)
+        lo, hi = halves(g.src)
+        incoming(g, base + 2, p, 2, lo)
+        incoming(g, base + 3, p, 2, hi)
+        share(g, p, 2)
+
+    for g in gathers:
+        launch(move(g, 0, 0, 0, g.a.plus, fresh=True))
+        launch(move(g, 1, 0, 0, g.a.minus, fresh=True))
+    for g in gathers:
+        spread(g, 0, fresh=True)
+        share(g, 0, 0, fresh=True)
     stores += [
         pltpu.make_async_copy(qm, mq_out, out_sem.at[4]),
         pltpu.make_async_copy(om, mo_out, out_sem.at[5]),
-        pltpu.make_async_copy(wq, wq_out.at[:, rows(me), :], out_sem.at[6]),
-        pltpu.make_async_copy(wo, wo_out.at[:, rows(me), :], out_sem.at[7]),
+        pltpu.make_async_copy(wq, place_of(GQ, 0, 0), out_sem.at[6]),
+        pltpu.make_async_copy(wo, place_of(GO, 0, 0), out_sem.at[7]),
     ]
     for copy in stores[4:]:
         copy.start()
+    for g in gathers:
+        lo, hi = halves(g.src)
+        incoming(g, 0, -1, 0)
+        launch(move(g, 2, -1, 0, g.a.plus, lo))
+        incoming(g, 1, 1, 0)
+        launch(move(g, 3, 1, 0, g.a.minus, hi))
+        spread(g, -1)
+        spread(g, 1)
+        share(g, -1, 0)
+        share(g, 1, 0)
+    for g in gathers:
+        relay(g, 0)
+    for g in gathers:
+        lo, hi = halves(g.src)
+        incoming(g, 2, 2, 0, lo)
+        incoming(g, 3, 2, 0, hi)
+        spread(g, 2)
+        share(g, 2, 0)
+    for p in (-1, 1, 2):
+        for g in gathers:
+            relay(g, p)
+    for p in (0, -1, 1, 2):
+        for g in gathers:
+            far(g, p)
+    for g in gathers:
+        for p in range(SIDE):
+            for q in range(SIDE):
+                n = number(p, q)
+                there = place_of(g, p, q, c=other)
+                remote(there, there, x_s.at[g.i, n], x_r.at[g.i, n], partner).wait_recv()
 
     def finish(k, _):
         d = peer(k)
-        for copy in w_copies(d, d):
-            copy.wait_recv()
-            copy.wait_send()
-        for copy in grad_copies(d, me):
-            copy.wait_send()
         g_copy(d, me).wait_send()
         p_copy(d, me).wait_send()
         n_copy(d, me).wait_send()
@@ -314,7 +490,19 @@
     lax.fori_loop(1, N, finish, 0)
     for j in range(1, GROUPS):
         z_copy(lax.rem(z + j, GROUPS), z).wait_send()
+    for copy in sent:
+        copy.wait_send()
     for copy in stores:
+        copy.wait()
+
+
+def emit(*refs):
+    count = (len(refs) - 1) // 2
+    sem = refs[-1]
+    copies = [pltpu.make_async_copy(refs[i], refs[count + i], sem.at[i]) for i in range(count)]
+    for copy in copies:
+        copy.start()
+    for copy in copies:
         copy.wait()
 
 
@@ -329,6 +517,17 @@
     anywhere = pl.BlockSpec(memory_space=pl.ANY)
     scalars = pl.BlockSpec(memory_space=pltpu.SMEM)
     dma = pltpu.SemaphoreType.DMA
+
+    def sum_scratch(r, w):
+        vm = pltpu.VMEM
+        chunk, piece = (r, SIDE, HEIGHT, w), (r, HEIGHT, w)
+        half = (r // 2, SIDE, HEIGHT, w), (r // 2, HEIGHT, w)
+        return (
+            vm((SIDE,) + chunk, bf16), vm((SIDE,) + chunk, bf16), vm((SIDE,) + chunk, f32),
+            vm((2,) + half[0], f32), vm((2,) + chunk, f32), vm((SIDE,) + piece, f32),
+            vm((2,) + half[1], f32), vm((2,) + piece, f32), vm(piece, f32),
+        )
+
     outs = pl.pallas_call(
         kernel,
         out_shape=[
@@ -336,18 +535,16 @@
             jax.ShapeDtypeStruct(opiece, f32),
             jax.ShapeDtypeStruct(qpiece, f32),
             jax.ShapeDtypeStruct(opiece, f32),
-            jax.ShapeDtypeStruct((8, BLK, 512), bf16),
-            jax.ShapeDtypeStruct((2, BLK, 2048), bf16),
+            jax.ShapeDtypeStruct((8, 16, 2, HEIGHT, 512), bf16),
+            jax.ShapeDtypeStruct((2, 16, 2, HEIGHT, 2048), bf16),
             jax.ShapeDtypeStruct(stat, f32),
             jax.ShapeDtypeStruct(stat, f32),
         ],
-        in_specs=[scalars, scalars] + [anywhere] * 10,
+        in_specs=[scalars, scalars] + [pl.BlockSpec(memory_space=pltpu.HBM)] * 10,
         out_specs=[anywhere] * 8,
         scratch_shapes=[
-            pltpu.VMEM((N,) + qpiece, bf16),
-            pltpu.VMEM((N,) + opiece, bf16),
-            pltpu.VMEM(qpiece, f32),
-            pltpu.VMEM(opiece, f32),
+            *sum_scratch(8, 512),
+            *sum_scratch(2, 2048),
             pltpu.VMEM((NB + 1, HEIGHT, BLK), f32),
             pltpu.VMEM((N, CAP, HEIGHT, BLK), f32),
             pltpu.VMEM(stat, f32),
@@ -370,16 +567,36 @@
             dma((8,)),
             dma((8,)),
         ]
-        + [dma((N,))] * 8
+        + [dma((2, SIDE))] * 3
+        + [dma((2, 6))] * 4
+        + [dma((N,))] * 4
         + [dma((GROUPS,))] * 2
-        + [dma((N,))] * 6,
-        compiler_params=pltpu.CompilerParams(collective_id=0, has_side_effects=True, vmem_limit_bytes=60 << 20),
+        + [dma((N,))] * 2
+        + [dma((2, 20))] * 2
+        + [dma((2, 16))] * 2,
+        compiler_params=pltpu.CompilerParams(collective_id=0, has_side_effects=True, vmem_limit_bytes=LIMIT << 20),
         name="shampoo",
     )(
-        source, key, grad_query, grad_output, query_master, output_master, query_moment, output_moment,
-        left_stat[0, 0], right_stat[0, 0], left_root[0, 0], right_root[0, 0],
+        source, key,
+        *(
+            pltpu.with_memory_space_constraint(x, pltpu.HBM)
+            for x in (
+                grad_query.reshape(1, 8, SIDE, SIDE, 2, HEIGHT, 512),
+                grad_output.reshape(1, 2, SIDE, SIDE, 2, HEIGHT, 2048),
+                query_master, output_master, query_moment, output_moment,
+                left_stat[0, 0], right_stat[0, 0], left_root[0, 0], right_root[0, 0],
+            )
+        ),
     )
-    mq, mo, vq, vo, wq, wo, ln, rn = outs
+    mq, mo, vq, vo, wq, wo, ln, rn = pl.pallas_call(
+        emit,
+        out_shape=[jax.ShapeDtypeStruct(x.shape, x.dtype) for x in outs],
+        in_specs=[anywhere] * 8,
+        out_specs=[pl.BlockSpec(memory_space=pltpu.HBM)] * 8,
+        scratch_shapes=[dma((8,))],
+        compiler_params=pltpu.CompilerParams(vmem_limit_bytes=1 << 20),
+        name="emit",
+    )(*outs)
     return mq, mo, vq, vo, wq.reshape(-1, 512), wo.reshape(-1, 2048), ln[None, None], rn[None, None]
 
 

time: 198 us -> 93.8 us (0.47)
  Pallas kernels: 181 us -> 90.7 us
  local copies, waits for them, and re-layouts: 12.9 us -> 0 us
    pallas_call x1, Pallas kernels: 181 us -> 88 us  [on_device(): pl.pallas_call(kernel, out_shape=[jax.ShapeDtypeStruct(qpiece, f32), jax....]
    unnamed x14 -> x0, local copies, waits for them, and re-layouts: 12.9 us -> none
    pallas_call x0 -> x1, Pallas kernels: none -> 2.74 us  [on_device(): pl.pallas_call(emit, out_shape=[jax.ShapeDtypeStruct(x.shape, x.dtype) fo...]
where the time goes in v2:
time: 93.8 us; the launch traced here: 93.7 us
  Pallas kernels  90.7 us (97%)
  other arithmetic  2.33 us (2%)
    pallas_call x1, Pallas kernels, on_device(): pl.pallas_call(kernel, out_shape=[jax.ShapeDtypeStruct(qpiece, f32), jax....  88 us
    pallas_call x1, Pallas kernels, on_device(): pl.pallas_call(emit, out_shape=[jax.ShapeDtypeStruct(x.shape, x.dtype) fo...  2.74 us

profile of v2, /device:TPU:1, one launch (start us, length us, event | category | flops | bytes accessed | tf_op | source)
XLA Modules:
  0.0 93.7 jit_solution(4178635085449144060)
XLA Ops:
  0.6 0.9 convert_reduce_fusion
  1.5 0.7 multiply_add_fusion.key
  2.2 0.7 fusion.1
  2.9 0.1 select_reduce_fusion
  3.0 88.0 %shampoo.1 = (f32[8,8,512]{2,1,0:T(8,128)S(1)}, f32[2,8,2048]{2,1,0:T(8,128)S(1)}, f32[8,8,512]{2,1,0:T(8,128)S(1)}, f32[2,8,2048]{2,1,0:T(8,128)S(1)}, bf16[8,1...) custom-call(s32[96]{0:T(128)S(1)} %broadcast_add_fusion.source, ...), custom_call_target="tpu_custom_call" | custom-call | tf_op jit(solution)/shard_map/shampoo/pallas_call | solution.py:531
  90.9 2.7 %emit.1 = (f32[8,8,512]{2,1,0:T(8,128)}, f32[2,8,2048]{2,1,0:T(8,128)}, f32[8,8,512]{2,1,0:T(8,128)}, f32[2,8,2048]{2,1,0:T(8,128)}, bf16[8,16,2,8,512]{4,3,2,1,...) custom-call(f32[8,8,512]{2,1,0:T(8,128)S(1)} %get-tuple-element.24.refs_0_, ...), custom_call_target="tpu_custom_call" | custom-call | tf_op jit(solution)/shard_map/emit/pallas_call | solution.py:591
  (2 shorter events, 0.0 us)

commit v3 on v2

--- a/solution.py
+++ b/solution.py
@@ -72,8 +72,17 @@
     row = me // (2 * SIDE)
     other = 1 - core
 
-    def peer(k):
-        return lax.rem(me + k, N)
+    def everyone(act):
+        def chip(j, _):
+            y = lax.rem(row + 2 + 3 * (j // SIDE), SIDE)
+            x = lax.rem(col + 2 + 3 * lax.rem(j, SIDE), SIDE)
+            for c in range(2):
+                act((y * SIDE + x) * 2 + lax.rem(core + c, 2))
+            return 0
+
+        lax.fori_loop(0, 10, chip, 0)
+        lax.fori_loop(11, 16, chip, 0)
+        act(row * 2 * SIDE + col * 2 + other)
 
     def device(y, x, c):
         return {"dp": (y * SIDE + x) * 2 + c}
@@ -120,16 +129,13 @@
 
     barrier = pltpu.get_barrier_semaphore()
 
-    def greet(k, _):
-        pl.semaphore_signal(barrier, inc=1, device_id={"dp": peer(k)}, device_id_type=MESH)
-        return 0
-
-    lax.fori_loop(1, N, greet, 0)
+    for to in (partner, east, west, south, north):
+        pl.semaphore_signal(barrier, inc=1, device_id=to, device_id_type=MESH)
     for j in range(1, GROUPS):
         pl.semaphore_signal(
             barrier, inc=1, device_id={"tensor": lax.rem(z + j, GROUPS)}, device_id_type=MESH
         )
-    pl.semaphore_wait(barrier, N - 1 + GROUPS - 1)
+    pl.semaphore_wait(barrier, 5 + GROUPS - 1)
 
     sent = []
 
@@ -138,82 +144,120 @@
         sent.append(copy)
         return copy
 
+    def raw_slice(a, k, q, c):
+        f, s = turn(a.f, k), turn(a.s, q)
+        y, x = (s, f) if a.query else (f, s)
+        return a.raw.at[0, :, y, x, c]
+
     pairs = {}
-    for k in order:
-        for a in both:
-            pairs[a.sems, k] = launch(
-                remote(raw_chunk(a, k, other), a.other.at[k], pair_s.at[a.sems, k], pair_r.at[a.sems, k], partner)
-            )
-
-    def pair_sum(a, k):
-        own_loads[a.sems, k].wait()
-        pairs[a.sems, k].wait_recv()
-        a.s1[k] = a.own[k].astype(jnp.float32) + a.other[k].astype(jnp.float32)
+    for q in order:
+        for k in order:
+            for a in both:
+                n = q * SIDE + k
+                pairs[a.sems, q, k] = launch(
+                    remote(
+                        raw_slice(a, k, q, other), a.other.at[k, :, turn(a.s, q)],
+                        pair_s.at[a.sems, n], pair_r.at[a.sems, n], partner,
+                    )
+                )
+
+    def pair_sum(a, k, q):
+        if q == order[0]:
+            own_loads[a.sems, k].wait()
+        pairs[a.sems, q, k].wait_recv()
+        s = turn(a.s, q)
+        a.s1[k, :, s] = a.own[k, :, s].astype(jnp.float32) + a.other[k, :, s].astype(jnp.float32)
 
     def chunk_copies(a, send, recv, piece, rl, rx, plus, minus):
-        lo, hi = halves(rx.at[0])
+        lo, hi = halves(a.total)
         return dict(
-            relay_plus=remote(piece(2, lo), rl.at[0], send.at[0], recv.at[0], plus),
-            relay_minus=remote(piece(2, hi), rl.at[1], send.at[1], recv.at[1], minus),
-            near_plus=remote(piece(1, hi), rx.at[0, hi], send.at[2], recv.at[2], plus),
-            near_minus=remote(piece(3, lo), rx.at[1, lo], send.at[3], recv.at[3], minus),
-            last_plus=remote(piece(1, lo), rx.at[0, lo], send.at[4], recv.at[4], plus),
-            last_minus=remote(piece(3, hi), rx.at[1, hi], send.at[5], recv.at[5], minus),
+            relay_plus=remote(piece(2, lo), rl(0), send.at[0], recv.at[0], plus),
+            relay_minus=remote(piece(2, hi), rl(1), send.at[1], recv.at[1], minus),
+            near_plus=remote(piece(1, hi), rx(0, hi), send.at[2], recv.at[2], plus),
+            near_minus=remote(piece(3, lo), rx(1, lo), send.at[3], recv.at[3], minus),
+            last_plus=remote(piece(1, lo), rx(0, lo), send.at[4], recv.at[4], plus),
+            last_minus=remote(piece(3, hi), rx(1, hi), send.at[5], recv.at[5], minus),
         )
 
     one, two = {}, {}
     for a in both:
         i = a.sems
-        one[i] = chunk_copies(
-            a, one_s.at[i], one_r.at[i], lambda k, r, a=a: a.s1.at[k, r], a.rl1, a.rx1, a.plus, a.minus
-        )
+        for q in order:
+            s = turn(a.s, q)
+            one[i, q] = chunk_copies(
+                a, one_s.at[i, q], one_r.at[i, q],
+                lambda k, r, a=a, s=s: a.s1.at[k, r, s],
+                lambda w, a=a, s=s: a.rl1.at[w, :, s],
+                lambda w, r, a=a, s=s: a.rx1.at[w, r, s],
+                a.plus, a.minus,
+            )
         two[i] = chunk_copies(
-            a, two_s.at[i], two_r.at[i], lambda k, r, a=a: a.t.at[turn(a.s, k), r], a.rl2, a.rx2, a.up, a.down
-        )
-
-    for a in both:
-        pair_sum(a, 2)
-        launch(one[a.sems]["relay_plus"])
-        launch(one[a.sems]["relay_minus"])
-    for a in both:
-        pair_sum(a, 1)
-        launch(one[a.sems]["near_plus"])
-    for a in both:
-        pair_sum(a, 3)
-        launch(one[a.sems]["near_minus"])
-    for a in both:
-        pair_sum(a, 0)
-    for a in both:
-        lo, hi = halves(a.s1.at[0])
-        one[a.sems]["relay_plus"].wait_recv()
-        a.s1[1, lo] += a.rl1[0]
-        launch(one[a.sems]["last_plus"])
-        one[a.sems]["relay_minus"].wait_recv()
-        a.s1[3, hi] += a.rl1[1]
-        launch(one[a.sems]["last_minus"])
-    for a in both:
-        for name in ("near_plus", "near_minus", "last_plus", "last_minus"):
-            one[a.sems][name].wait_recv()
-        for k in (2, 1, 3, 0):
-            s = turn(a.s, k)
+            a, two_s.at[i], two_r.at[i],
+            lambda k, r, a=a: a.t.at[turn(a.s, k), r],
+            lambda w, a=a: a.rl2.at[w],
+            lambda w, r, a=a: a.rx2.at[w, r],
+            a.up, a.down,
+        )
+
+    def open_slice(q):
+        for a in both:
+            pair_sum(a, 2, q)
+            launch(one[a.sems, q]["relay_plus"])
+            launch(one[a.sems, q]["relay_minus"])
+        for a in both:
+            pair_sum(a, 1, q)
+            launch(one[a.sems, q]["near_plus"])
+            pair_sum(a, 3, q)
+            launch(one[a.sems, q]["near_minus"])
+
+    def pass_slice(q):
+        for a in both:
+            lo, hi = halves(a.total)
+            s = turn(a.s, q)
+            one[a.sems, q]["relay_plus"].wait_recv()
+            a.s1[1, lo, s] += a.rl1[0, :, s]
+            launch(one[a.sems, q]["last_plus"])
+            one[a.sems, q]["relay_minus"].wait_recv()
+            a.s1[3, hi, s] += a.rl1[1, :, s]
+            launch(one[a.sems, q]["last_minus"])
+            pair_sum(a, 0, q)
+
+    def close_slice(q):
+        for a in both:
+            s = turn(a.s, q)
+            for name in ("near_plus", "near_minus", "last_plus", "last_minus"):
+                one[a.sems, q][name].wait_recv()
             a.t[s] = a.s1[0, :, s] + a.rx1[0, :, s] + a.rx1[1, :, s]
-            if k == 2:
+            if q == 2:
                 launch(two[a.sems]["relay_plus"])
                 launch(two[a.sems]["relay_minus"])
-            elif k == 1:
+            elif q == 1:
                 launch(two[a.sems]["near_plus"])
-            elif k == 3:
+            elif q == 3:
                 launch(two[a.sems]["near_minus"])
-    for a in both:
-        lo, hi = halves(a.t.at[0])
-        s = turn(a.s, 1)
-        two[a.sems]["relay_plus"].wait_recv()
-        a.t[s, lo] += a.rl2[0]
-        launch(two[a.sems]["last_plus"])
-        s = turn(a.s, 3)
-        two[a.sems]["relay_minus"].wait_recv()
-        a.t[s, hi] += a.rl2[1]
-        launch(two[a.sems]["last_minus"])
+
+    def pass_on(name, last, k, half):
+        for a in both:
+            s = turn(a.s, k)
+            r = halves(a.total)[half]
+            two[a.sems][name].wait_recv()
+            a.t[s, r] += a.rl2[half]
+            launch(two[a.sems][last])
+
+    open_slice(2)
+    open_slice(1)
+    pass_slice(2)
+    open_slice(3)
+    pass_slice(1)
+    close_slice(2)
+    open_slice(0)
+    pass_slice(3)
+    close_slice(1)
+    pass_on("relay_plus", "last_plus", 1, 0)
+    pass_slice(0)
+    close_slice(3)
+    pass_on("relay_minus", "last_minus", 3, 1)
+    close_slice(0)
     for a in both:
         for name in ("near_plus", "near_minus", "last_plus", "last_minus"):
             two[a.sems][name].wait_recv()
@@ -230,12 +274,9 @@
             blocks[QB + r * 8 + c] = so[r, :, c * BLK : (c + 1) * BLK]
     blocks[NB] = jnp.zeros((HEIGHT, BLK), jnp.float32)
 
-    def place(d, _):
+    def place(d):
         for s in range(CAP):
             gsend[d, s] = blocks[source[d * CAP + s]]
-        return 0
-
-    lax.fori_loop(0, N, place, 0)
 
     def g_copy(to, slot):
         return pltpu.make_async_remote_copy(
@@ -243,11 +284,12 @@
             device_id={"dp": to}, device_id_type=MESH,
         )
 
-    def send_blocks(k, _):
-        g_copy(peer(k), me).start()
-        return 0
-
-    lax.fori_loop(1, N, send_blocks, 0)
+    def send_blocks(d):
+        place(d)
+        g_copy(d, me).start()
+
+    everyone(send_blocks)
+    place(me)
     own_g = pltpu.make_async_copy(gsend.at[me], gfull.at[:, rows(me), :], g_r.at[me])
     own_g.start()
 
@@ -259,8 +301,8 @@
     ov[...] = fresh_o
     adam_q = sq[...] / (jnp.sqrt(fresh_q) + adam_eps)
     adam_o = so[...] / (jnp.sqrt(fresh_o) + adam_eps)
-    adam_q2 = jnp.sum(adam_q * adam_q)
-    adam_o2 = jnp.sum(adam_o * adam_o)
+    adam_q2 = jnp.sum(jnp.sum(adam_q * adam_q, axis=0), axis=(0, 1), keepdims=True)
+    adam_o2 = jnp.sum(jnp.sum(adam_o * adam_o, axis=0), axis=(0, 1), keepdims=True)
     stores = [
         pltpu.make_async_copy(qv, vq_out, out_sem.at[0]),
         pltpu.make_async_copy(ov, vo_out, out_sem.at[1]),
@@ -270,12 +312,7 @@
 
     own_g.wait()
 
-    def wait_blocks(k, _):
-        frm = peer(k)
-        g_copy(frm, frm).wait_recv()
-        return 0
-
-    lax.fori_loop(1, N, wait_blocks, 0)
+    everyone(lambda d: g_copy(d, d).wait_recv())
 
     loads[0].wait()
     loads[1].wait()
@@ -283,15 +320,17 @@
     def dot(a, b, dims=((1,), (0,))):
         return lax.dot_general(a, b, (dims, ((), ())), precision=highest, preferred_element_type=jnp.float32)
 
-    prec_q2 = 0.0
-    prec_o2 = 0.0
+    prec_q2 = jnp.zeros((1, BLK), jnp.float32)
+    prec_o2 = jnp.zeros((1, BLK), jnp.float32)
     for s in range(CAP):
         pre = dot(dot(lr[s], gfull[s]), rr[s])
         pbuf[s] = pre
-        square = jnp.sum(pre * pre)
+        square = jnp.sum(pre * pre, axis=0, keepdims=True)
         is_query = source[me * CAP + s] < QB
         prec_q2 = prec_q2 + jnp.where(is_query, square, 0.0)
         prec_o2 = prec_o2 + jnp.where(is_query, 0.0, square)
+    prec_q2 = jnp.sum(prec_q2, axis=1, keepdims=True)
+    prec_o2 = jnp.sum(prec_o2, axis=1, keepdims=True)
 
     def p_copy(to, slot):
         return pltpu.make_async_remote_copy(
@@ -299,15 +338,9 @@
             device_id={"dp": to}, device_id_type=MESH,
         )
 
-    def send_prec(k, _):
-        p_copy(peer(k), me).start()
-        return 0
-
-    lax.fori_loop(1, N, send_prec, 0)
     own_p = pltpu.make_async_copy(pbuf.at[:, rows(me), :], prec.at[pl.ds(me * CAP, CAP)], p_r.at[me])
-    own_p.start()
-
-    lane = lax.broadcasted_iota(jnp.int32, (8, 128), 1)
+
+    lane = lax.broadcasted_iota(jnp.int32, (1, 128), 1)
     mine = jnp.where(lane == 0, adam_q2, jnp.where(lane == 1, adam_o2, jnp.where(lane == 2, prec_q2, prec_o2)))
     znorm[...] = mine
 
@@ -319,8 +352,8 @@
     for j in range(1, GROUPS):
         z_copy(lax.rem(z + j, GROUPS), z).start()
 
-    loads[6].wait()
-    loads[7].wait()
+    everyone(lambda d: p_copy(d, me).start())
+    own_p.start()
     znet[z] = mine
     for j in range(1, GROUPS):
         frm = lax.rem(z + j, GROUPS)
@@ -333,13 +366,11 @@
             nsend, nnet.at[slot], n_s.at[to], n_r.at[slot], device_id={"dp": to}, device_id_type=MESH
         )
 
-    def send_norm(k, _):
-        n_copy(peer(k), me).start()
-        return 0
-
-    lax.fori_loop(1, N, send_norm, 0)
+    everyone(lambda d: n_copy(d, me).start())
     nnet[me] = total
 
+    loads[6].wait()
+    loads[7].wait()
     for s in range(CAP):
         g = gfull[s]
         ls[s] = stat_decay * ls[s] + (1.0 - stat_decay) * dot(g, g, ((1,), (1,)))
@@ -353,36 +384,21 @@
 
     own_p.wait()
 
-    def wait_prec(k, _):
-        frm = peer(k)
-        p_copy(frm, frm).wait_recv()
-        n_copy(frm, frm).wait_recv()
-        return 0
-
-    lax.fori_loop(1, N, wait_prec, 0)
+    def wait_prec(d):
+        p_copy(d, d).wait_recv()
+        n_copy(d, d).wait_recv()
+
+    everyone(wait_prec)
     norms = jnp.sum(nnet[...], axis=0)
 
     def pick(i):
-        return jnp.sum(jnp.where(lane == i, norms, 0.0), axis=1, keepdims=True)[0:1]
+        return jnp.sum(jnp.where(lane == i, norms, 0.0), axis=1, keepdims=True)
 
     scale_q = learn_rate * (jnp.sqrt(pick(0)) / (jnp.sqrt(pick(2)) + graft_eps))
     scale_o = learn_rate * (jnp.sqrt(pick(1)) / (jnp.sqrt(pick(3)) + graft_eps))
 
     loads[4].wait()
     loads[5].wait()
-    for r in range(8):
-        for c in range(2):
-            cols = slice(c * BLK, (c + 1) * BLK)
-            fresh = qm[r, :, cols] - scale_q * prec[key[r * 2 + c]]
-            qm[r, :, cols] = fresh
-            wq[r, :, cols] = fresh.astype(jnp.bfloat16)
-    for r in range(2):
-        for c in range(8):
-            cols = slice(c * BLK, (c + 1) * BLK)
-            fresh = om[r, :, cols] - scale_o * prec[key[QB + r * 8 + c]]
-            om[r, :, cols] = fresh
-            wo[r, :, cols] = fresh.astype(jnp.bfloat16)
-
     class Gather:
         pass
 
@@ -435,10 +451,26 @@
         incoming(g, base + 3, p, 2, hi)
         share(g, p, 2)
 
-    for g in gathers:
+    def masters_query():
+        for r in range(8):
+            for c in range(2):
+                cols = slice(c * BLK, (c + 1) * BLK)
+                fresh = qm[r, :, cols] - scale_q * prec[key[r * 2 + c]]
+                qm[r, :, cols] = fresh
+                wq[r, :, cols] = fresh.astype(jnp.bfloat16)
+
+    def masters_output():
+        for r in range(2):
+            for c in range(8):
+                cols = slice(c * BLK, (c + 1) * BLK)
+                fresh = om[r, :, cols] - scale_o * prec[key[QB + r * 8 + c]]
+                om[r, :, cols] = fresh
+                wo[r, :, cols] = fresh.astype(jnp.bfloat16)
+
+    for g, masters in ((GQ, masters_query), (GO, masters_output)):
+        masters()
         launch(move(g, 0, 0, 0, g.a.plus, fresh=True))
         launch(move(g, 1, 0, 0, g.a.minus, fresh=True))
-    for g in gathers:
         spread(g, 0, fresh=True)
         share(g, 0, 0, fresh=True)
     stores += [
@@ -455,6 +487,7 @@
         launch(move(g, 2, -1, 0, g.a.plus, lo))
         incoming(g, 1, 1, 0)
         launch(move(g, 3, 1, 0, g.a.minus, hi))
+    for g in gathers:
         spread(g, -1)
         spread(g, 1)
         share(g, -1, 0)
@@ -480,14 +513,12 @@
                 there = place_of(g, p, q, c=other)
                 remote(there, there, x_s.at[g.i, n], x_r.at[g.i, n], partner).wait_recv()
 
-    def finish(k, _):
-        d = peer(k)
+    def finish(d):
         g_copy(d, me).wait_send()
         p_copy(d, me).wait_send()
         n_copy(d, me).wait_send()
-        return 0
-
-    lax.fori_loop(1, N, finish, 0)
+
+    everyone(finish)
     for j in range(1, GROUPS):
         z_copy(lax.rem(z + j, GROUPS), z).wait_send()
     for copy in sent:
@@ -560,15 +591,16 @@
             pltpu.VMEM(stat, f32),
             pltpu.VMEM(qpiece, bf16),
             pltpu.VMEM(opiece, bf16),
-            pltpu.VMEM((8, 128), f32),
-            pltpu.VMEM((GROUPS, 8, 128), f32),
-            pltpu.VMEM((8, 128), f32),
-            pltpu.VMEM((N, 8, 128), f32),
+            pltpu.VMEM((1, 128), f32),
+            pltpu.VMEM((GROUPS, 1, 128), f32),
+            pltpu.VMEM((1, 128), f32),
+            pltpu.VMEM((N, 1, 128), f32),
             dma((8,)),
             dma((8,)),
         ]
-        + [dma((2, SIDE))] * 3
-        + [dma((2, 6))] * 4
+        + [dma((2, SIDE)), dma((2, 16)), dma((2, 16))]
+        + [dma((2, SIDE, 6))] * 2
+        + [dma((2, 6))] * 2
         + [dma((N,))] * 4
         + [dma((GROUPS,))] * 2
         + [dma((N,))] * 2

time: 93.8 us -> 90.8 us (0.968)
  Pallas kernels: 90.7 us -> 87.7 us
    pallas_call x1, Pallas kernels: 88 us -> 84.9 us  [on_device(): pl.pallas_call(kernel, out_shape=[jax.ShapeDtypeStruct(qpiece, f32), jax....]
where the time goes in v3:
time: 90.8 us; the launch traced here: 90.6 us
  Pallas kernels  87.7 us (97%)
  other arithmetic  2.33 us (3%)
    pallas_call x1, Pallas kernels, on_device(): pl.pallas_call(kernel, out_shape=[jax.ShapeDtypeStruct(qpiece, f32), jax....  84.9 us
    pallas_call x1, Pallas kernels, on_device(): pl.pallas_call(emit, out_shape=[jax.ShapeDtypeStruct(x.shape, x.dtype) fo...  2.74 us

profile of v3, /device:TPU:1, one launch (start us, length us, event | category | flops | bytes accessed | tf_op | source)
XLA Modules:
  0.0 90.6 jit_solution(643518690291702497)
XLA Ops:
  0.6 0.9 %convert_reduce_fusion = s32[32]{0:T(128)S(1)} fusion(s32[32]{0:T(128)} %bitcast.28), kind=kLoop, calls=%fused_computation.2 | loop fusion | flops 5088 | bytes 256 | tf_op jit(solution)/shard_map/reduce_sum | solution.py:32
  1.5 0.7 multiply_add_fusion.key
  2.2 0.7 fusion.1
  2.9 0.1 select_reduce_fusion
  3.0 84.9 %shampoo.1 = (f32[8,8,512]{2,1,0:T(8,128)S(1)}, f32[2,8,2048]{2,1,0:T(8,128)S(1)}, f32[8,8,512]{2,1,0:T(8,128)S(1)}, f32[2,8,2048]{2,1,0:T(8,128)S(1)}, bf16[8,1...) custom-call(s32[96]{0:T(128)S(1)} %broadcast_add_fusion.source, ...), custom_call_target="tpu_custom_call" | custom-call | tf_op jit(solution)/shard_map/shampoo/pallas_call | solution.py:562
  87.9 2.7 %emit.1 = (f32[8,8,512]{2,1,0:T(8,128)}, f32[2,8,2048]{2,1,0:T(8,128)}, f32[8,8,512]{2,1,0:T(8,128)}, f32[2,8,2048]{2,1,0:T(8,128)}, bf16[8,16,2,8,512]{4,3,2,1,...) custom-call(f32[8,8,512]{2,1,0:T(8,128)S(1)} %get-tuple-element.24.refs_0_, ...), custom_call_target="tpu_custom_call" | custom-call | tf_op jit(solution)/shard_map/emit/pallas_call | solution.py:623
  (2 shorter events, 0.0 us)

commit v4 on v3

--- a/solution.py
+++ b/solution.py
@@ -14,7 +14,7 @@
 NB = 32
 QB = 16
 HEIGHT = BLK // N
-LIMIT = 36
+LIMIT = 30
 
 highest = lax.Precision.HIGHEST
 stat_decay = 0.99
@@ -26,16 +26,6 @@
 MESH = pl.DeviceIdType.MESH
 
 
-def tables(owner_row):
-    ids = jnp.arange(NB, dtype=jnp.int32)
-    same = owner_row[:, None] == owner_row[None, :]
-    slot = jnp.sum((same & (ids[None, :] < ids[:, None])).astype(jnp.int32), axis=1)
-    key = owner_row * CAP + slot
-    places = jnp.arange(N * CAP, dtype=jnp.int32)
-    source = NB + jnp.sum(jnp.where(key[None, :] == places[:, None], ids[None, :] - NB, 0), axis=1)
-    return source, key
-
-
 SIDE = 4
 
 
@@ -45,9 +35,6 @@
         self.own, self.other, self.s1, self.rl1, self.rx1, self.t, self.rl2, self.rx2, self.total = refs
         self.sems = sems
 
-    def at(self, ref, f, s=slice(None), r=slice(None)):
-        return ref.at[r, s, f] if self.query else ref.at[r, f, s]
-
 
 def halves(ref):
     rows = ref.shape[0]
@@ -55,15 +42,15 @@
 
 
 def kernel(
-    source, key, gq, go, qmast, omast, qmom, omom, lstat, rstat, lroot, rroot,
+    owner, gq, go, qmast, omast, qmom, omom, lstat, rstat, lroot, rroot,
     mq_out, mo_out, vq_out, vo_out, wq_out, wo_out, ln_out, rn_out,
     q_own, q_oth, q_s1, q_rl1, q_rx1, q_t, q_rl2, q_rx2, sq,
     o_own, o_oth, o_s1, o_rl1, o_rx1, o_t, o_rl2, o_rx2, so,
     blocks, gsend, gfull, pbuf, prec,
     qm, om, qv, ov, ls, rs, lr, rr, wq, wo,
-    znorm, znet, nsend, nnet,
-    in_sem, out_sem, own_sem, pair_s, pair_r, one_s, one_r, two_s, two_r,
-    g_s, g_r, p_s, p_r, z_s, z_r, n_s, n_r, w_s, w_r, x_s, x_r,
+    znorm, znet, nsend, nnet, own_row, own_words, line, key, source,
+    in_sem, out_sem, table_sem, own_sem, first_r, pair_s, pair_r, one_s, one_r, two_s, two_r,
+    few_s, few_r, w_s, w_r, x_s, x_r,
 ):
     me = lax.axis_index("dp")
     z = lax.axis_index("tensor")
@@ -97,6 +84,16 @@
     def remote(src, dst, send, recv, to):
         return pltpu.make_async_remote_copy(src, dst, send, recv, device_id=to, device_id_type=MESH)
 
+    def arrived(ref, sem):
+        remote(ref, ref, sem, sem, partner).wait_recv()
+
+    def left(ref, sem):
+        remote(ref, ref, sem, sem, partner).wait_send()
+
+    read_row = pltpu.make_async_copy(owner, own_row, table_sem.at[0])
+    read_words = pltpu.make_async_copy(owner, own_words, table_sem.at[1])
+    read_row.start()
+    read_words.start()
     Q = Grads(True, gq, (q_own, q_oth, q_s1, q_rl1, q_rx1, q_t, q_rl2, q_rx2, sq), 0)
     O = Grads(False, go, (o_own, o_oth, o_s1, o_rl1, o_rx1, o_t, o_rl2, o_rx2, so), 1)
     Q.f, Q.s, O.f, O.s = col, row, row, col
@@ -105,19 +102,12 @@
     both = (Q, O)
     order = (2, 1, 3, 0)
 
-    def raw_chunk(a, k, c):
-        f = turn(a.f, k)
-        if a.query:
-            return a.raw.at[0, :, :, f, c]
-        return a.raw.at[0, :, f, :, c]
-
-    own_loads = {}
-    for k in order:
-        for a in both:
-            own_loads[a.sems, k] = pltpu.make_async_copy(
-                raw_chunk(a, k, core), a.own.at[k], own_sem.at[a.sems, k]
-            )
-            own_loads[a.sems, k].start()
+    own_loads = []
+    for a in both:
+        for f in range(SIDE):
+            src = a.raw.at[0, :, :, f, core] if a.query else a.raw.at[0, :, f, :, core]
+            own_loads.append(pltpu.make_async_copy(src, a.own.at[f], own_sem.at[a.sems, f]))
+            own_loads[-1].start()
     loads = [
         pltpu.make_async_copy(src, dst, in_sem.at[i])
         for i, (src, dst) in enumerate(
@@ -135,13 +125,30 @@
         pl.semaphore_signal(
             barrier, inc=1, device_id={"tensor": lax.rem(z + j, GROUPS)}, device_id_type=MESH
         )
+
+    lanes = lax.broadcasted_iota(jnp.int32, (1, 128), 1)
+    read_row.wait()
+    read_words.wait()
+    row_of = own_row[...]
+    spot = lanes[:, :NB]
+    slot = jnp.zeros((1, NB), jnp.int32)
+    for b in range(NB):
+        slot = slot + jnp.where((row_of == own_words[0, b]) & (spot > b), 1, 0)
+    line[0:1, 0:NB] = row_of * CAP + slot
+    put_key = pltpu.make_async_copy(line.at[0:1], key, table_sem.at[2])
+    put_key.start()
+    put_key.wait()
+    found = jnp.full((1, 128), NB, jnp.int32)
+    for b in range(NB):
+        found = jnp.where(lanes == key[0, b], b, found)
+    line[1:2, :] = found
+    put_source = pltpu.make_async_copy(line.at[1:2], source, table_sem.at[3])
+    put_source.start()
+    put_source.wait()
     pl.semaphore_wait(barrier, 5 + GROUPS - 1)
-
-    sent = []
 
     def launch(copy):
         copy.start()
-        sent.append(copy)
         return copy
 
     def raw_slice(a, k, q, c):
@@ -149,34 +156,39 @@
         y, x = (s, f) if a.query else (f, s)
         return a.raw.at[0, :, y, x, c]
 
+    first = order[0]
     pairs = {}
-    for q in order:
+
+    def pair_slice(q):
         for k in order:
             for a in both:
-                n = q * SIDE + k
+                recv = first_r.at[a.sems, k] if q == first else pair_r.at[a.sems, q]
                 pairs[a.sems, q, k] = launch(
                     remote(
-                        raw_slice(a, k, q, other), a.other.at[k, :, turn(a.s, q)],
-                        pair_s.at[a.sems, n], pair_r.at[a.sems, n], partner,
+                        raw_slice(a, k, q, other), a.other.at[k, :, turn(a.s, q)], pair_s.at[a.sems], recv, partner
                     )
                 )
 
     def pair_sum(a, k, q):
-        if q == order[0]:
-            own_loads[a.sems, k].wait()
-        pairs[a.sems, q, k].wait_recv()
-        s = turn(a.s, q)
-        a.s1[k, :, s] = a.own[k, :, s].astype(jnp.float32) + a.other[k, :, s].astype(jnp.float32)
+        s, f = turn(a.s, q), turn(a.f, k)
+        if q == first:
+            if k == first:
+                for copy in own_loads[a.sems * SIDE : (a.sems + 1) * SIDE]:
+                    copy.wait()
+            pairs[a.sems, q, k].wait_recv()
+        elif k == first:
+            arrived(a.other.at[:, :, s], pair_r.at[a.sems, q])
+        a.s1[k, :, s] = a.own[f, :, s].astype(jnp.float32) + a.other[k, :, s].astype(jnp.float32)
 
     def chunk_copies(a, send, recv, piece, rl, rx, plus, minus):
         lo, hi = halves(a.total)
         return dict(
-            relay_plus=remote(piece(2, lo), rl(0), send.at[0], recv.at[0], plus),
-            relay_minus=remote(piece(2, hi), rl(1), send.at[1], recv.at[1], minus),
-            near_plus=remote(piece(1, hi), rx(0, hi), send.at[2], recv.at[2], plus),
-            near_minus=remote(piece(3, lo), rx(1, lo), send.at[3], recv.at[3], minus),
-            last_plus=remote(piece(1, lo), rx(0, lo), send.at[4], recv.at[4], plus),
-            last_minus=remote(piece(3, hi), rx(1, hi), send.at[5], recv.at[5], minus),
+            relay_plus=remote(piece(2, lo), rl(0), send, recv.at[0], plus),
+            relay_minus=remote(piece(2, hi), rl(1), send, recv.at[0], minus),
+            near_plus=remote(piece(1, hi), rx(0, hi), send, recv.at[1], plus),
+            near_minus=remote(piece(3, lo), rx(1, lo), send, recv.at[1], minus),
+            last_plus=remote(piece(1, lo), rx(0, lo), send, recv.at[1], plus),
+            last_minus=remote(piece(3, hi), rx(1, hi), send, recv.at[1], minus),
         )
 
     one, two = {}, {}
@@ -185,7 +197,7 @@
         for q in order:
             s = turn(a.s, q)
             one[i, q] = chunk_copies(
-                a, one_s.at[i, q], one_r.at[i, q],
+                a, one_s.at[i], one_r.at[i, q],
                 lambda k, r, a=a, s=s: a.s1.at[k, r, s],
                 lambda w, a=a, s=s: a.rl1.at[w, :, s],
                 lambda w, r, a=a, s=s: a.rx1.at[w, r, s],
@@ -214,10 +226,9 @@
         for a in both:
             lo, hi = halves(a.total)
             s = turn(a.s, q)
-            one[a.sems, q]["relay_plus"].wait_recv()
+            arrived(a.rl1.at[:, :, s], one_r.at[a.sems, q, 0])
             a.s1[1, lo, s] += a.rl1[0, :, s]
             launch(one[a.sems, q]["last_plus"])
-            one[a.sems, q]["relay_minus"].wait_recv()
             a.s1[3, hi, s] += a.rl1[1, :, s]
             launch(one[a.sems, q]["last_minus"])
             pair_sum(a, 0, q)
@@ -225,8 +236,7 @@
     def close_slice(q):
         for a in both:
             s = turn(a.s, q)
-            for name in ("near_plus", "near_minus", "last_plus", "last_minus"):
-                one[a.sems, q][name].wait_recv()
+            arrived(a.rx1.at[:, :, s], one_r.at[a.sems, q, 1])
             a.t[s] = a.s1[0, :, s] + a.rx1[0, :, s] + a.rx1[1, :, s]
             if q == 2:
                 launch(two[a.sems]["relay_plus"])
@@ -236,16 +246,21 @@
             elif q == 3:
                 launch(two[a.sems]["near_minus"])
 
-    def pass_on(name, last, k, half):
+    def pass_on(last, k, half):
         for a in both:
             s = turn(a.s, k)
             r = halves(a.total)[half]
-            two[a.sems][name].wait_recv()
+            if half == 0:
+                arrived(a.rl2, two_r.at[a.sems, 0])
             a.t[s, r] += a.rl2[half]
             launch(two[a.sems][last])
 
+    pair_slice(2)
+    pair_slice(1)
     open_slice(2)
+    pair_slice(3)
     open_slice(1)
+    pair_slice(0)
     pass_slice(2)
     open_slice(3)
     pass_slice(1)
@@ -253,14 +268,13 @@
     open_slice(0)
     pass_slice(3)
     close_slice(1)
-    pass_on("relay_plus", "last_plus", 1, 0)
+    pass_on("last_plus", 1, 0)
     pass_slice(0)
     close_slice(3)
-    pass_on("relay_minus", "last_minus", 3, 1)
+    pass_on("last_minus", 3, 1)
     close_slice(0)
     for a in both:
-        for name in ("near_plus", "near_minus", "last_plus", "last_minus"):
-            two[a.sems][name].wait_recv()
+        arrived(a.rx2, two_r.at[a.sems, 1])
         a.total[...] = a.t[a.s] + a.rx2[0] + a.rx2[1]
 
     def rows(d):
@@ -276,11 +290,11 @@
 
     def place(d):
         for s in range(CAP):
-            gsend[d, s] = blocks[source[d * CAP + s]]
+            gsend[d, s] = blocks[source[0, d * CAP + s]]
 
     def g_copy(to, slot):
         return pltpu.make_async_remote_copy(
-            gsend.at[to], gfull.at[:, rows(slot), :], g_s.at[to], g_r.at[slot],
+            gsend.at[to], gfull.at[:, rows(slot), :], few_s.at[0], few_r.at[0],
             device_id={"dp": to}, device_id_type=MESH,
         )
 
@@ -290,7 +304,7 @@
 
     everyone(send_blocks)
     place(me)
-    own_g = pltpu.make_async_copy(gsend.at[me], gfull.at[:, rows(me), :], g_r.at[me])
+    own_g = pltpu.make_async_copy(gsend.at[me], gfull.at[:, rows(me), :], few_r.at[0])
     own_g.start()
 
     loads[2].wait()
@@ -310,9 +324,7 @@
     for copy in stores:
         copy.start()
 
-    own_g.wait()
-
-    everyone(lambda d: g_copy(d, d).wait_recv())
+    arrived(gfull, few_r.at[0])
 
     loads[0].wait()
     loads[1].wait()
@@ -326,7 +338,7 @@
         pre = dot(dot(lr[s], gfull[s]), rr[s])
         pbuf[s] = pre
         square = jnp.sum(pre * pre, axis=0, keepdims=True)
-        is_query = source[me * CAP + s] < QB
+        is_query = source[0, me * CAP + s] < QB
         prec_q2 = prec_q2 + jnp.where(is_query, square, 0.0)
         prec_o2 = prec_o2 + jnp.where(is_query, 0.0, square)
     prec_q2 = jnp.sum(prec_q2, axis=1, keepdims=True)
@@ -334,11 +346,11 @@
 
     def p_copy(to, slot):
         return pltpu.make_async_remote_copy(
-            pbuf.at[:, rows(to), :], prec.at[pl.ds(slot * CAP, CAP)], p_s.at[to], p_r.at[slot],
+            pbuf.at[:, rows(to), :], prec.at[pl.ds(slot * CAP, CAP)], few_s.at[1], few_r.at[1],
             device_id={"dp": to}, device_id_type=MESH,
         )
 
-    own_p = pltpu.make_async_copy(pbuf.at[:, rows(me), :], prec.at[pl.ds(me * CAP, CAP)], p_r.at[me])
+    own_p = pltpu.make_async_copy(pbuf.at[:, rows(me), :], prec.at[pl.ds(me * CAP, CAP)], few_r.at[1])
 
     lane = lax.broadcasted_iota(jnp.int32, (1, 128), 1)
     mine = jnp.where(lane == 0, adam_q2, jnp.where(lane == 1, adam_o2, jnp.where(lane == 2, prec_q2, prec_o2)))
@@ -346,7 +358,7 @@
 
     def z_copy(to, slot):
         return pltpu.make_async_remote_copy(
-            znorm, znet.at[slot], z_s.at[to], z_r.at[slot], device_id={"tensor": to}, device_id_type=MESH
+            znorm, znet.at[slot], few_s.at[2], few_r.at[2], device_id={"tensor": to}, device_id_type=MESH
         )
 
     for j in range(1, GROUPS):
@@ -355,15 +367,13 @@
     everyone(lambda d: p_copy(d, me).start())
     own_p.start()
     znet[z] = mine
-    for j in range(1, GROUPS):
-        frm = lax.rem(z + j, GROUPS)
-        z_copy(frm, frm).wait_recv()
+    arrived(znet.at[pl.ds(0, GROUPS - 1)], few_r.at[2])
     total = znet[0] + znet[1] + znet[2] + znet[3]
     nsend[...] = total
 
     def n_copy(to, slot):
         return pltpu.make_async_remote_copy(
-            nsend, nnet.at[slot], n_s.at[to], n_r.at[slot], device_id={"dp": to}, device_id_type=MESH
+            nsend, nnet.at[slot], few_s.at[3], few_r.at[3], device_id={"dp": to}, device_id_type=MESH
         )
 
     everyone(lambda d: n_copy(d, me).start())
@@ -382,13 +392,8 @@
     stores[2].start()
     stores[3].start()
 
-    own_p.wait()
-
-    def wait_prec(d):
-        p_copy(d, d).wait_recv()
-        n_copy(d, d).wait_recv()
-
-    everyone(wait_prec)
+    arrived(prec, few_r.at[1])
+    arrived(nnet.at[pl.ds(0, N - 1)], few_r.at[3])
     norms = jnp.sum(nnet[...], axis=0)
 
     def pick(i):
@@ -413,49 +418,41 @@
 
     def move(g, n, p, q, to, r=slice(None), fresh=False):
         src = g.src.at[r] if fresh else place_of(g, p, q, r)
-        return remote(src, place_of(g, p, q, r), w_s.at[g.i, n], w_r.at[g.i, n], to)
-
-    def incoming(g, n, p, q, r=slice(None)):
-        there = place_of(g, p, q, r)
-        remote(there, there, w_s.at[g.i, n], w_r.at[g.i, n], partner).wait_recv()
-
-    def number(p, q):
-        return (p % SIDE) * SIDE + q % SIDE
+        return remote(src, place_of(g, p, q, r), w_s.at[g.i], w_r.at[g.i, n], to)
+
+    def incoming(g, n, p, q):
+        arrived(place_of(g, p, q), w_r.at[g.i, n])
 
     def share(g, p, q, fresh=False):
         src = g.src if fresh else place_of(g, p, q)
-        n = number(p, q)
-        launch(remote(src, place_of(g, p, q), x_s.at[g.i, n], x_r.at[g.i, n], partner))
+        launch(remote(src, place_of(g, p, q), x_s.at[g.i], x_r.at[g.i], partner))
 
     gathers = (GQ, GO)
 
     def spread(g, p, fresh=False):
-        base = 4 + 4 * (p % SIDE)
+        base = 3 + 3 * (p % SIDE)
         launch(move(g, base + 0, p, 0, g.a.up, fresh=fresh))
         launch(move(g, base + 1, p, 0, g.a.down, fresh=fresh))
 
     def relay(g, p):
-        base = 4 + 4 * (p % SIDE)
+        base = 3 + 3 * (p % SIDE)
         lo, hi = halves(g.src)
         incoming(g, base + 0, p, -1)
         launch(move(g, base + 2, p, -1, g.a.up, lo))
+        incoming(g, base + 1, p, 1)
+        launch(move(g, base + 2, p, 1, g.a.down, hi))
         share(g, p, -1)
-        incoming(g, base + 1, p, 1)
-        launch(move(g, base + 3, p, 1, g.a.down, hi))
         share(g, p, 1)
 
     def far(g, p):
-        base = 4 + 4 * (p % SIDE)
-        lo, hi = halves(g.src)
-        incoming(g, base + 2, p, 2, lo)
-        incoming(g, base + 3, p, 2, hi)
+        incoming(g, 5 + 3 * (p % SIDE), p, 2)
         share(g, p, 2)
 
     def masters_query():
         for r in range(8):
             for c in range(2):
                 cols = slice(c * BLK, (c + 1) * BLK)
-                fresh = qm[r, :, cols] - scale_q * prec[key[r * 2 + c]]
+                fresh = qm[r, :, cols] - scale_q * prec[key[0, r * 2 + c]]
                 qm[r, :, cols] = fresh
                 wq[r, :, cols] = fresh.astype(jnp.bfloat16)
 
@@ -463,7 +460,7 @@
         for r in range(2):
             for c in range(8):
                 cols = slice(c * BLK, (c + 1) * BLK)
-                fresh = om[r, :, cols] - scale_o * prec[key[QB + r * 8 + c]]
+                fresh = om[r, :, cols] - scale_o * prec[key[0, QB + r * 8 + c]]
                 om[r, :, cols] = fresh
                 wo[r, :, cols] = fresh.astype(jnp.bfloat16)
 
@@ -486,7 +483,7 @@
         incoming(g, 0, -1, 0)
         launch(move(g, 2, -1, 0, g.a.plus, lo))
         incoming(g, 1, 1, 0)
-        launch(move(g, 3, 1, 0, g.a.minus, hi))
+        launch(move(g, 2, 1, 0, g.a.minus, hi))
     for g in gathers:
         spread(g, -1)
         spread(g, 1)
@@ -495,9 +492,7 @@
     for g in gathers:
         relay(g, 0)
     for g in gathers:
-        lo, hi = halves(g.src)
-        incoming(g, 2, 2, 0, lo)
-        incoming(g, 3, 2, 0, hi)
+        incoming(g, 2, 2, 0)
         spread(g, 2)
         share(g, 2, 0)
     for p in (-1, 1, 2):
@@ -507,22 +502,18 @@
         for g in gathers:
             far(g, p)
     for g in gathers:
-        for p in range(SIDE):
-            for q in range(SIDE):
-                n = number(p, q)
-                there = place_of(g, p, q, c=other)
-                remote(there, there, x_s.at[g.i, n], x_r.at[g.i, n], partner).wait_recv()
-
-    def finish(d):
-        g_copy(d, me).wait_send()
-        p_copy(d, me).wait_send()
-        n_copy(d, me).wait_send()
-
-    everyone(finish)
-    for j in range(1, GROUPS):
-        z_copy(lax.rem(z + j, GROUPS), z).wait_send()
-    for copy in sent:
-        copy.wait_send()
+        arrived(g.dst.at[:, :, other], x_r.at[g.i])
+    for a in both:
+        left(a.other, pair_s.at[a.sems])
+        left(a.s1.at[pl.ds(1, SIDE - 1)], one_s.at[a.sems])
+        left(a.t.at[pl.ds(1, SIDE - 1)], two_s.at[a.sems])
+    left(gsend.at[pl.ds(0, N - 1)], few_s.at[0])
+    left(prec.at[pl.ds(0, (N - 1) * CAP)], few_s.at[1])
+    left(znet.at[pl.ds(0, GROUPS - 1)], few_s.at[2])
+    left(nnet.at[pl.ds(0, N - 1)], few_s.at[3])
+    for g in gathers:
+        left(g.dst.at[:, pl.ds(0, 15), core], w_s.at[g.i])
+        left(g.dst.at[:, :, core], x_s.at[g.i])
     for copy in stores:
         copy.wait()
 
@@ -541,12 +532,10 @@
     grad_query, grad_output, query_master, output_master, query_moment, output_moment,
     left_stat, right_stat, left_root, right_root, owner,
 ):
-    source, key = tables(owner[0])
     f32, bf16 = jnp.float32, jnp.bfloat16
     stat = (CAP, BLK, BLK)
     qpiece, opiece = query_master.shape, output_master.shape
     anywhere = pl.BlockSpec(memory_space=pl.ANY)
-    scalars = pl.BlockSpec(memory_space=pltpu.SMEM)
     dma = pltpu.SemaphoreType.DMA
 
     def sum_scratch(r, w):
@@ -571,7 +560,7 @@
             jax.ShapeDtypeStruct(stat, f32),
             jax.ShapeDtypeStruct(stat, f32),
         ],
-        in_specs=[scalars, scalars] + [pl.BlockSpec(memory_space=pltpu.HBM)] * 10,
+        in_specs=[pl.BlockSpec(memory_space=pltpu.HBM)] * 11,
         out_specs=[anywhere] * 8,
         scratch_shapes=[
             *sum_scratch(8, 512),
@@ -595,25 +584,36 @@
             pltpu.VMEM((GROUPS, 1, 128), f32),
             pltpu.VMEM((1, 128), f32),
             pltpu.VMEM((N, 1, 128), f32),
+            pltpu.VMEM((1, NB), jnp.int32),
+            pltpu.SMEM((1, NB), jnp.int32),
+            pltpu.VMEM((2, 128), jnp.int32),
+            pltpu.SMEM((1, 128), jnp.int32),
+            pltpu.SMEM((1, 128), jnp.int32),
             dma((8,)),
             dma((8,)),
-        ]
-        + [dma((2, SIDE)), dma((2, 16)), dma((2, 16))]
-        + [dma((2, SIDE, 6))] * 2
-        + [dma((2, 6))] * 2
-        + [dma((N,))] * 4
-        + [dma((GROUPS,))] * 2
-        + [dma((N,))] * 2
-        + [dma((2, 20))] * 2
-        + [dma((2, 16))] * 2,
+            dma((4,)),
+            dma((2, SIDE)),
+            dma((2, SIDE)),
+            dma((2,)),
+            dma((2, SIDE)),
+            dma((2,)),
+            dma((2, SIDE, 2)),
+            dma((2,)),
+            dma((2, 2)),
+            dma((4,)),
+            dma((4,)),
+            dma((2,)),
+            dma((2, 15)),
+            dma((2,)),
+            dma((2,)),
+        ],
         compiler_params=pltpu.CompilerParams(collective_id=0, has_side_effects=True, vmem_limit_bytes=LIMIT << 20),
         name="shampoo",
     )(
-        source, key,
         *(
             pltpu.with_memory_space_constraint(x, pltpu.HBM)
             for x in (
-                grad_query.reshape(1, 8, SIDE, SIDE, 2, HEIGHT, 512),
+                owner, grad_query.reshape(1, 8, SIDE, SIDE, 2, HEIGHT, 512),
                 grad_output.reshape(1, 2, SIDE, SIDE, 2, HEIGHT, 2048),
                 query_master, output_master, query_moment, output_moment,
                 left_stat[0, 0], right_stat[0, 0], left_root[0, 0], right_root[0, 0],

time: 90.8 us -> 82.9 us (0.913)
  Pallas kernels: 87.7 us -> 82.1 us
  other arithmetic: 2.33 us -> 0 us
    pallas_call x1, Pallas kernels: 84.9 us -> 79.4 us  [on_device(): pl.pallas_call(kernel, out_shape=[jax.ShapeDtypeStruct(qpiece, f32), jax....]
    reduce_sum x2 -> x0, other arithmetic: 1 us -> none  [the longest x1 0.91 us: tables(): jnp.sum((same & (ids[None, :] < ids[:, None])).astype(jnp.int32), axis=1)]
where the time goes in v4:
time: 82.9 us; the launch traced here: 82.8 us
  Pallas kernels  82.1 us (99%)
    pallas_call x1, Pallas kernels, on_device(): pl.pallas_call(kernel, out_shape=[jax.ShapeDtypeStruct(qpiece, f32), jax....  79.4 us
    pallas_call x1, Pallas kernels, on_device(): pl.pallas_call(emit, out_shape=[jax.ShapeDtypeStruct(x.shape, x.dtype) fo...  2.74 us

profile of v4, /device:TPU:1, one launch (start us, length us, event | category | flops | bytes accessed | tf_op | source)
XLA Modules:
  0.0 82.8 jit_solution(17480445614847662508)
XLA Ops:
  0.6 79.4 %shampoo.1 = (f32[8,8,512]{2,1,0:T(8,128)S(1)}, f32[2,8,2048]{2,1,0:T(8,128)S(1)}, f32[8,8,512]{2,1,0:T(8,128)S(1)}, f32[2,8,2048]{2,1,0:T(8,128)S(1)}, bf16[8,1...) custom-call(s32[1,32]{1,0:T(1,128)} %owner.1, ...), custom_call_target="tpu_custom_call" | custom-call | tf_op jit(solution)/shard_map/shampoo/pallas_call | solution.py:551
  80.0 2.7 %emit.1 = (f32[8,8,512]{2,1,0:T(8,128)}, f32[2,8,2048]{2,1,0:T(8,128)}, f32[8,8,512]{2,1,0:T(8,128)}, f32[2,8,2048]{2,1,0:T(8,128)}, bf16[8,16,2,8,512]{4,3,2,1,...) custom-call(f32[8,8,512]{2,1,0:T(8,128)S(1)} %get-tuple-element.24.refs_0_, ...), custom_call_target="tpu_custom_call" | custom-call | tf_op jit(solution)/shard_map/emit/pallas_call | solution.py:623
